TPU v7x, 256 devices: a whole 4x4x8 slice. The times are simulated.
256 devices in a mesh: seq: 32 (over y, z), head: 8 (over x, core).
Axes of the slice: x: 4, y: 4, z: 8, core: 2. Of those that a mesh axis runs over, the one named last changes fastest.
Arguments:
- tokens: bfloat16 [16384, 2048], P('seq'), may hold values from -24 to 24
- w_query: bfloat16 [2048, 2048], P(None, 'head'), may hold values from -0.125 to 0.125
- w_key: bfloat16 [2048, 2048], P(None, 'head'), may hold values from -0.125 to 0.125
- w_value: bfloat16 [2048, 2048], P(None, 'head'), may hold values from -0.125 to 0.125
- w_out: bfloat16 [2048, 2048], P('head'), may hold values from -0.125 to 0.125
- shared_gate: bfloat16 [2048, 1024], P(None, 'head'), may hold values from -0.125 to 0.125
- shared_up: bfloat16 [2048, 1024], P(None, 'head'), may hold values from -0.125 to 0.125
- shared_down: bfloat16 [1024, 2048], P('head'), may hold values from -0.1875 to 0.1875
- expert_gate: bfloat16 [64, 2048, 1024], P('seq', None, 'head'), may hold values from -0.125 to 0.125
- expert_up: bfloat16 [64, 2048, 1024], P('seq', None, 'head'), may hold values from -0.125 to 0.125
- expert_down: bfloat16 [64, 1024, 2048], P('seq', 'head'), may hold values from -0.1875 to 0.1875
- expert_ids: int32 [16384, 1], P('seq'), may hold values from 0 to 63; in each aligned block of 512 rows (0 to 511, 512 to 1023, ...) at most 16 rows name the same one
Outputs:
- output: bfloat16 [16384, 2048], P('seq', 'head')
Inputs may be any that keep to these rules, and one draw needn't show every extreme that they name: `expert_ids`: among the 512 tokens of one index of seq (aligned blocks of the sequence) at most 16 name the same expert, and in some block of every draw one expert is named by exactly 16 tokens.
All inputs are finite; a program needn't handle non-finite values.
Results may differ from a plain program's by a relative error of at most 0.015.
Values may be sent and summed in bfloat16 or wider, within the bound.
A program may use at most 128 MiB of HBM per device.

v0:
```python
import jax
import jax.numpy as jnp
from jax import lax
from jax.sharding import PartitionSpec as P

HD = 128
EXPERTS = 64
CAP = 16


def prefix(array, axis, combine, identity):
    length, mine = (lax.axis_size(axis), lax.axis_index(axis))
    everything = lax.all_gather(array, axis)
    start = jnp.broadcast_to(jnp.asarray(identity, array.dtype), array.shape)

    def hop(k, before):
        reached = k < mine
        new = combine(before, everything[k])
        return jnp.where(reached, new, before)

    return lax.fori_loop(0, length, hop, start)


def rms_rows(values):
    return values * lax.rsqrt(jnp.mean(values * values, axis=-1, keepdims=True) + 1e-06)


def add_states(earlier, later):
    return earlier + later


def causal_attention(query_rows, key_rows, value_rows):
    row_count = query_rows.shape[0]
    block_rows = min(512, row_count)
    causal = jnp.arange(block_rows)[:, None] >= jnp.arange(block_rows)[None, :]
    block_states = [
        jnp.einsum("thd,the->hde", key_rows, value_rows, preferred_element_type=jnp.float32)
    ]
    local_state = block_states[0]
    return (local_state, block_rows, causal, block_states)


def shards(
    tokens,
    w_query,
    w_key,
    w_value,
    w_out,
    shared_gate,
    shared_up,
    shared_down,
    expert_gate,
    expert_up,
    expert_down,
    expert_ids,
):
    highest = lax.Precision.HIGHEST
    rows_here = tokens.shape[0]
    model_width = tokens.shape[1]
    heads_here = w_query.shape[1] // HD
    experts_here = expert_gate.shape[0]
    inputs = tokens.astype(jnp.float32)
    normed_input = rms_rows(inputs).astype(jnp.bfloat16)
    query_rows = (
        jnp.dot(normed_input, w_query, preferred_element_type=jnp.float32)
        .astype(jnp.bfloat16)
        .reshape(rows_here, heads_here, HD)
    )
    key_rows = (
        jnp.dot(normed_input, w_key, preferred_element_type=jnp.float32)
        .astype(jnp.bfloat16)
        .reshape(rows_here, heads_here, HD)
    )
    value_rows = (
        jnp.dot(normed_input, w_value, preferred_element_type=jnp.float32)
        .astype(jnp.bfloat16)
        .reshape(rows_here, heads_here, HD)
    )
    local_state, block_rows, causal, block_states = causal_attention(
        query_rows, key_rows, value_rows
    )
    carried = prefix(local_state, "seq", add_states, jnp.zeros_like(local_state))
    scores = jnp.einsum("thd,shd->hts", query_rows, key_rows, preferred_element_type=jnp.float32)
    scores = jnp.where(causal[None], scores, 0.0)
    within = jnp.einsum("hts,shd->thd", scores, value_rows.astype(jnp.float32), precision=highest)
    before = jnp.einsum("thd,hde->the", query_rows.astype(jnp.float32), carried, precision=highest)
    outputs = within + before
    head_normed = rms_rows(outputs).reshape(rows_here, heads_here * HD).astype(jnp.bfloat16)
    head_term = jnp.dot(head_normed, w_out, preferred_element_type=jnp.float32)
    col_width = model_width // lax.axis_size("head")
    head_position = lax.axis_index("head")
    summed = lax.psum(head_term.astype(jnp.bfloat16), "head").astype(jnp.float32)
    residual = inputs + summed
    normed_mid = rms_rows(residual).astype(jnp.bfloat16)
    residual_share = lax.dynamic_slice_in_dim(residual, head_position * col_width, col_width, 1)
    expert_of = expert_ids[:, 0]
    onehot = (expert_of[:, None] == jnp.arange(EXPERTS, dtype=jnp.int32)[None, :]).astype(jnp.int32)
    slot_rank = jnp.sum(jnp.cumsum(onehot, axis=0) * onehot, axis=1) - 1
    slot_index = expert_of * CAP + slot_rank
    source_row = (
        jnp.full((EXPERTS * CAP,), rows_here, jnp.int32)
        .at[slot_index]
        .set(jnp.arange(rows_here, dtype=jnp.int32))
    )
    padded = jnp.concatenate([normed_mid, jnp.zeros((1, model_width), jnp.bfloat16)], axis=0)
    outgoing = jnp.take(padded, source_row, axis=0).reshape(EXPERTS, CAP, model_width)
    arrived = lax.all_to_all(outgoing, "seq", split_axis=0, concat_axis=0, tiled=True)
    sources = arrived.shape[0] // experts_here
    count = arrived.shape[1]
    grouped = arrived.reshape(sources, experts_here, count, model_width)
    gate_act = jnp.einsum(
        "secd,edf->secf", grouped, expert_gate, preferred_element_type=jnp.float32
    )
    up_act = jnp.einsum("secd,edf->secf", grouped, expert_up, preferred_element_type=jnp.float32)
    hidden = (jax.nn.silu(gate_act) * up_act).astype(jnp.bfloat16)
    result = jnp.einsum(
        "secf,efd->secd", hidden, expert_down, preferred_element_type=jnp.float32
    ).astype(jnp.bfloat16)
    result = result.reshape(arrived.shape[0], count, model_width)
    returned = lax.all_to_all(result, "seq", split_axis=0, concat_axis=0, tiled=True)
    returned_width = returned.shape[2]
    routed = jnp.take(returned.reshape(EXPERTS * CAP, returned_width), slot_index, axis=0)
    shared_hidden = (
        jax.nn.silu(jnp.dot(normed_mid, shared_gate, preferred_element_type=jnp.float32))
        * jnp.dot(normed_mid, shared_up, preferred_element_type=jnp.float32)
    ).astype(jnp.bfloat16)
    shared_term = jnp.dot(shared_hidden, shared_down, preferred_element_type=jnp.float32)
    shared_total, routed_sum = (
        lax.psum_scatter(
            shared_term.astype(jnp.bfloat16), "head", scatter_dimension=1, tiled=True
        ).astype(jnp.float32),
        lax.psum_scatter(
            routed.astype(jnp.float32).astype(jnp.bfloat16), "head", scatter_dimension=1, tiled=True
        ).astype(jnp.float32),
    )
    routed_total = routed_sum.astype(jnp.bfloat16)
    return (residual_share + shared_total + routed_total.astype(jnp.float32)).astype(jnp.bfloat16)


def solution(mesh):
    return jax.shard_map(
        shards,
        mesh=mesh,
        in_specs=(
            P("seq", None),
            P(None, "head"),
            P(None, "head"),
            P(None, "head"),
            P("head", None),
            P(None, "head"),
            P(None, "head"),
            P("head", None),
            P("seq", None, "head"),
            P("seq", None, "head"),
            P("seq", "head", None),
            P("seq", None),
        ),
        out_specs=P("seq", "head"),
        check_vma=False,
    )
```

profile of v0, /device:TPU:1, one launch (start us, length us, event | category | flops | bytes accessed | tf_op | source)
XLA Modules:
  0.0 490.1 jit_solution(9188890959421161135)
XLA Ops:
  6.5 2.2 fusion
  8.8 2.7 convolution_convert_fusion.2
  14.2 1.2 reduce-window.6
  16.2 2.1 convolution_convert_fusion.3
  19.0 1.8 fusion.59
  20.8 75.5 %all-gather.3.cloned.1.call-done = f32[64,128,128]{2,1,0:T(8,128)} async-done(((f32[2,128,128]{2,1,0:T(8,128)}), f32[64,128,128]{2,1,0:T(8,128)}) %all-gather.3.cloned.1.call-update) | async-done | bytes 4194320 | tf_op jit(solution)/shard_map/all_gather | solution.py:13
  96.3 31.1 %while.14 = (s32[]{:T(128)}, f32[2,128,128]{2,1,0:T(8,128)S(1)}, s32[]{:T(128)}, f32[32,2,128,128]{3,2,1,0:T(8,128)}, s32[]{:T(128)}, /*index=5*/s32[]{:T(128)}) while((s32[]{:T(128)}, f32[2,128,128]{2,1,0:T(8,128)S(1)}, s32[]{:T(128)}, f32[32,2,128,128]{3,2,1,0:T(8,128)}, s32[]{:T(128)}, /*index=5*/s32[]{:T(128)}) %tuple.46), condition=%wide.region_2.3_spmd.clone, body=%wide.region_1.2_spmd.clone.sunk | while | flops 98308 | bytes 393317 | solution.py:21
  97.2 0.9 add_select_fusion.2
  98.2 0.9 add_select_fusion.2
  99.2 0.9 add_select_fusion.2
  127.4 1.5 fusion.61
  128.9 3.1 multiply_reduce_fusion.1
  132.1 2.1 convolution_convert_fusion.1
  134.6 2.4 scatter_custom_fusion
  137.2 66.3 %all-reduce.3.cloned.1.call-done = bf16[512,2048]{1,0:T(8,128)(2,1)} async-done(((bf16[512,2048]{1,0:T(8,128)(2,1)}), bf16[512,2048]{1,0:T(8,128)(2,1)}) %all-reduce.3.cloned.1.call-update) | async-done | bytes 2097168 | tf_op jit(solution)/shard_map/psum | solution.py:92
  203.5 4.3 convert_add_fusion
  208.5 1.4 copy-done.1
  210.1 6.0 %gather_fusion = bf16[1024,2048]{1,0:T(8,128)(2,1)} fusion(bf16[513,2048]{1,0:T(8,128)(2,1)S(1)} %concatenate.3, s32[1024]{0:T(1024)S(1)} %fusion.50), kind=kCustom, calls=%fused_computation | custom fusion | bytes 8392704 | tf_op jit(solution)/shard_map/jit(_take)/gather | solution.py:106
  216.2 2.6 broadcast_select_fusion
  218.8 100.4 %all_to_all.10 = bf16[64,16,2048]{2,1,0:T(8,128)(2,1)S(1)} all-to-all(bf16[64,16,2048]{2,1,0:T(8,128)(2,1)S(1)} %broadcast_select_fusion), channel_id=1, replica_groups=mesh['seq'=32,'head'=8] {'seq'}, dimensions={0} | all-to-all | bytes 8388608 | tf_op jit(solution)/shard_map/all_to_all | solution.py:107
  319.3 2.0 copy-done.5
  321.2 1.2 fusion.14
  322.5 6.5 %convert_bitcast_fusion = bf16[32,2,16,2048]{3,2,0,1:T(8,128)(2,1)} fusion(bf16[32,2,16,2048]{3,2,1,0:T(8,128)(2,1)} %bitcast.83, bf16[2,128,2048]{2,1,0:T(8,128)(2,1)S(1)} %copy-done, bf16[2,2048,128]{2,1,0:T(8,128)(2,1)S(1)} %copy-done.14, f32[32,2,16,128]{3,2,0,1:T(8,128)S(1)} %fusion.14), kind=kOutput, calls=%fused_computation.9 | convolution fusion | flops 1076625408 | bytes 11010048 | tf_op jit(solution)/shard_map/secf,efd->secd/dot_general | solution.py:116
  329.0 4.7 copy.30
  333.8 7.9 %all-to-all-start.1 = ((bf16[64,16,2048]{2,1,0:T(8,128)(2,1)}), bf16[64,16,2048]{2,1,0:T(8,128)(2,1)}, u32[]{:S(2)}, u32[]{:S(2)}) async-start(bf16[64,16,2048]{2,1,0:T(8,128)(2,1)} %bitcast.81), calls=%async_computation.2 | async-start | bytes 8388608 | tf_op jit(solution)/shard_map/all_to_all | solution.py:120
  341.7 1.8 fusion.62
  343.5 4.9 convolution_convert_fusion
  348.4 84.9 %all-to-all-done.1 = bf16[64,16,2048]{2,1,0:T(8,128)(2,1)} async-done(((bf16[64,16,2048]{2,1,0:T(8,128)(2,1)}), bf16[64,16,2048]{2,1,0:T(8,128)(2,1)}, u32[]{:S(2)}, u32[]{:S(2)}) %all-to-all-start.1) | async-done | bytes 4194336 | tf_op jit(solution)/shard_map/all_to_all | solution.py:120
  433.3 7.1 %gather_fusion.1 = bf16[512,2048]{1,0:T(8,128)(2,1)S(1)} fusion(bf16[1024,2048]{1,0:T(8,128)(2,1)} %bitcast.23, s32[1024]{0:T(1024)S(1)} %pad_clamp_fusion), kind=kCustom, calls=%fused_computation.1 | custom fusion | bytes 4196352 | tf_op jit(solution)/shard_map/jit(_take)/gather | solution.py:122
  440.5 1.6 broadcast_select_fusion.1
  442.1 39.5 %reduce-scatter.5.cloned.1.call-done = bf16[512,256]{1,0:T(8,128)(2,1)} async-done(((bf16[512,2048]{1,0:T(8,128)(2,1)}), bf16[512,256]{1,0:T(8,128)(2,1)}) %reduce-scatter.5.cloned.1.call-update) | async-done | bytes 262160 | tf_op jit(solution)/shard_map/reduce_scatter | solution.py:132
  481.6 2.0 add_convert_fusion
  (88 shorter events, 33.3 us)
Async XLA Ops:
  6.5 316.0 %copy-start = (bf16[2,128,2048]{2,1,0:T(8,128)(2,1)S(1)}, bf16[2,128,2048]{2,1,0:T(8,128)(2,1)}, u32[]{:S(2)}) copy-start(bf16[2,128,2048]{2,1,0:T(8,128)(2,1)} %param.24) | copy-start | bytes 3145732
  6.5 5.0 %copy-start.3 = (bf16[512,2048]{1,0:T(8,128)(2,1)S(1)}, bf16[512,2048]{1,0:T(8,128)(2,1)}, u32[]{:S(2)}) copy-start(bf16[512,2048]{1,0:T(8,128)(2,1)} %param.14) | copy-start | bytes 6291460
  6.5 89.7 %all-gather.3.cloned.1.call-start = ((), (), s32[]{:S(2)}) async-start(), calls=%async_computation.7 | async-start | bytes 4325376 | tf_op jit(solution)/shard_map/all_gather | solution.py:13
  6.5 5.0 %copy-start.12 = (bf16[2048,256]{1,0:T(8,128)(2,1)S(1)}, bf16[2048,256]{1,0:T(8,128)(2,1)}, u32[]{:S(2)}) copy-start(bf16[2048,256]{1,0:T(8,128)(2,1)} %param.17) | copy-start | bytes 3145732
  8.8 5.4 %copy-start.11 = (s32[512,1]{0,1:T(1,128)S(1)}, s32[512,1]{0,1:T(1,128)}, u32[]{:S(2)}) copy-start(s32[512,1]{0,1:T(1,128)} %param.25) | copy-start | bytes 6148
  11.5 1.0 copy-start.8
  12.5 0.7 copy-start.7
  14.1 189.5 %all-reduce.3.cloned.1.call-start = ((), (), s32[]{:S(2)}) async-start(), calls=%async_computation.4 | async-start | bytes 4194304 | tf_op jit(solution)/shard_map/psum | solution.py:92
  15.4 3.6 copy-start.9
  18.3 0.7 copy-start.6
  127.4 4.7 copy-start.10
  203.5 4.3 copy-start.4
  208.5 1.4 copy-start.1
  218.8 102.4 %copy-start.13 = (bf16[2,2048,128]{2,1,0:T(8,128)(2,1)S(1)}, bf16[2,2048,128]{2,1,0:T(8,128)(2,1)}, u32[]{:S(2)}) copy-start(bf16[2,2048,128]{2,1,0:T(8,128)(2,1)} %param.22) | copy-start | bytes 3145732
  319.3 2.0 copy-start.5
  319.3 3.2 copy-start.14
  333.8 8.0 %copy-start.2 = (bf16[512,2048]{1,0:T(8,128)(2,1)S(1)}, bf16[512,2048]{1,0:T(8,128)(2,1)}, u32[]{:S(2)}) copy-start(bf16[512,2048]{1,0:T(8,128)(2,1)} %copy-done.1) | copy-start | bytes 6291460
  333.8 99.6 %all-to-all-start.1 = ((bf16[64,16,2048]{2,1,0:T(8,128)(2,1)}), bf16[64,16,2048]{2,1,0:T(8,128)(2,1)}, u32[]{:S(2)}, u32[]{:S(2)}) async-start(bf16[64,16,2048]{2,1,0:T(8,128)(2,1)} %bitcast.81), calls=%async_computation.2 | async-start | bytes 8388608 | tf_op jit(solution)/shard_map/all_to_all | solution.py:120
  341.7 100.5 %reduce-scatter.3.cloned.1.call-start = ((), (), s32[]{:S(2)}) async-start(), calls=%async_computation.5 | async-start | bytes 2359296 | tf_op jit(solution)/shard_map/reduce_scatter | solution.py:129
  348.4 133.2 %reduce-scatter.5.cloned.1.call-start = ((), (), s32[]{:S(2)}) async-start(), calls=%async_computation.6 | async-start | bytes 2359296 | tf_op jit(solution)/shard_map/reduce_scatter | solution.py:132
Sparse Core Ops, SparseCore 0:
  14.2 82.0 all-gather.2
  134.3 69.1 all-reduce.2
  348.5 39.6 reduce-scatter.2
  442.2 39.3 reduce-scatter.4
where the time goes:
time: 493 us; the launch traced here: 490 us
  waiting for transfers between devices  266 us (54%)
  blocking collectives  100 us (20%)
  other arithmetic  46.1 us (9%)
  matrix products  29.4 us (6%)
  local copies, waits for them, and re-layouts  25.7 us (5%)
  between operations  13.5 us (3%)
  starting transfers between devices  8.02 us (2%)
    all_to_all x1, blocking collectives, shards(): lax.all_to_all(outgoing, 'seq', split_axis=0, concat_axis=0, tiled=True)  100 us
    all_to_all x1, waiting for transfers between devices, shards(): lax.all_to_all(result, 'seq', split_axis=0, concat_axis=0, tiled=True)  84.9 us
    all_gather x1, waiting for transfers between devices, prefix(): everything = lax.all_gather(array, axis)  75.5 us
    psum x1, waiting for transfers between devices, shards(): lax.psum(head_term.astype(jnp.bfloat16), 'head').astype(jnp.float32)  66.3 us
    reduce_scatter x1, waiting for transfers between devices, shards(): lax.psum_scatter(routed.astype(jnp.float32).astype(jnp.bfloat16), 'head',...  39.5 us
    select_n x32, other arithmetic, hop(): return jnp.where(reached, new, before)  30.4 us
  transfers between devices with their start and end apart: 5, of which 4 were waited for; matrix products, arithmetic and copies ran while one was open for 5% of the time, Pallas kernels for 0%

commit v1 on v0

v1 whole, which is shorter than its diff:
```python
import jax
import jax.numpy as jnp
from jax import lax
from jax.sharding import PartitionSpec as P

HD = 128
EXPERTS = 64
CAP = 16
F32 = jnp.float32
BF16 = jnp.bfloat16


def dot(a, b):
    return jnp.dot(a, b, preferred_element_type=F32)


def two_part(values):
    high = values.astype(BF16)
    return high, (values - high.astype(F32)).astype(BF16)


def head_columns(weights):
    return lax.all_to_all(weights, "head", split_axis=1, concat_axis=0, tiled=True)


def gather_columns(block):
    return lax.all_gather(block, "head", axis=1, tiled=True)


def carried_state(local_state):
    shape = local_state.shape
    length = lax.axis_size("seq")
    chunks = local_state.reshape(length, -1, HD)
    mine = lax.all_to_all(chunks, "seq", split_axis=0, concat_axis=0, tiled=True)
    earlier = jnp.arange(length)[:, None] > jnp.arange(length)[None, :]
    before = jnp.sum(jnp.where(earlier[:, :, None, None], mine[None], 0.0), axis=1)
    back = lax.all_to_all(before, "seq", split_axis=0, concat_axis=0, tiled=True)
    return back.reshape(shape)


def row_scale(rows):
    wide = rows.astype(F32)
    return lax.rsqrt(jnp.mean(wide * wide, axis=-1, keepdims=True) + 1e-06)


def shards(
    tokens,
    w_query,
    w_key,
    w_value,
    w_out,
    shared_gate,
    shared_up,
    shared_down,
    expert_gate,
    expert_up,
    expert_down,
    expert_ids,
):
    rows, width = tokens.shape
    heads = w_query.shape[1] // HD
    owned = expert_gate.shape[0]
    sources = lax.axis_size("seq")
    experts = owned * sources
    cols = width // lax.axis_size("head")
    head = lax.axis_index("head")

    out_cols = head_columns(w_out)
    shared_cols = head_columns(shared_down)
    expert_cols = lax.all_to_all(expert_down, "head", split_axis=2, concat_axis=1, tiled=True)

    inputs = tokens.astype(F32)
    normed = (inputs * row_scale(tokens)).astype(BF16)
    query = dot(normed, w_query).astype(BF16).reshape(rows, heads, HD)
    key = dot(normed, w_key).astype(BF16).reshape(rows, heads, HD)
    value = dot(normed, w_value).astype(BF16).reshape(rows, heads, HD)
    state = jnp.einsum("thd,the->hde", key, value, preferred_element_type=F32)
    carried = carried_state(state)
    causal = jnp.arange(rows)[:, None] >= jnp.arange(rows)[None, :]
    scores = jnp.einsum("thd,shd->hts", query, key, preferred_element_type=F32)
    scores = two_part(jnp.where(causal[None], scores, 0.0))
    carried = two_part(carried)
    attended = sum(
        jnp.einsum("hts,shd->thd", part, value, preferred_element_type=F32) for part in scores
    ) + sum(
        jnp.einsum("thd,hde->the", query, part, preferred_element_type=F32) for part in carried
    )
    head_normed = (
        attended * lax.rsqrt(jnp.mean(attended * attended, axis=-1, keepdims=True) + 1e-06)
    ).astype(BF16).reshape(rows, heads * HD)

    own_tokens = lax.dynamic_slice_in_dim(tokens, head * cols, cols, 1)
    residual = own_tokens.astype(F32) + dot(gather_columns(head_normed), out_cols)
    sent = residual.astype(BF16)

    expert_of = expert_ids[:, 0]
    same = (expert_of[:, None] == expert_of[None, :]) & causal
    rank = jnp.sum(same.astype(jnp.int32), axis=1) - 1
    slot = expert_of * CAP + rank
    chosen = jnp.arange(experts * CAP, dtype=jnp.int32)[:, None] == slot[None, :]
    chosen = chosen.astype(BF16)
    outgoing = dot(chosen, sent).astype(BF16).reshape(sources, owned, CAP, cols)
    arrived = lax.all_to_all(outgoing, "seq", split_axis=0, concat_axis=0, tiled=True)
    arrived = arrived.transpose(1, 0, 2, 3).reshape(owned * sources * CAP, cols)
    routed_in = gather_columns(arrived)

    middle = gather_columns(sent)
    scale = row_scale(middle)
    shared_hidden = (
        jax.nn.silu(dot(middle, shared_gate) * scale) * (dot(middle, shared_up) * scale)
    ).astype(BF16)

    scale = row_scale(routed_in).reshape(owned, sources * CAP, 1)
    routed_in = routed_in.reshape(owned, sources * CAP, width)
    gate = jnp.einsum("erd,edf->erf", routed_in, expert_gate, preferred_element_type=F32)
    up = jnp.einsum("erd,edf->erf", routed_in, expert_up, preferred_element_type=F32)
    routed_hidden = (jax.nn.silu(gate * scale) * (up * scale)).astype(BF16)
    both = jnp.concatenate([shared_hidden, routed_hidden.reshape(owned * sources * CAP, -1)])
    both = gather_columns(both)
    shared_out = dot(both[:rows], shared_cols)
    routed_out = jnp.einsum(
        "erf,efd->erd",
        both[rows:].reshape(owned, sources * CAP, -1),
        expert_cols,
        preferred_element_type=F32,
    ).astype(BF16)
    routed_out = routed_out.reshape(owned, sources, CAP, cols).transpose(1, 0, 2, 3)
    returned = lax.all_to_all(routed_out, "seq", split_axis=0, concat_axis=0, tiled=True)
    returned = returned.reshape(experts * CAP, cols)
    routed = lax.dot_general(
        chosen, returned, (((0,), (0,)), ((), ())), preferred_element_type=F32
    )
    return (residual + shared_out + routed).astype(BF16)


def solution(mesh):
    return jax.shard_map(
        shards,
        mesh=mesh,
        in_specs=(
            P("seq", None),
            P(None, "head"),
            P(None, "head"),
            P(None, "head"),
            P("head", None),
            P(None, "head"),
            P(None, "head"),
            P("head", None),
            P("seq", None, "head"),
            P("seq", None, "head"),
            P("seq", "head", None),
            P("seq", None),
        ),
        out_specs=P("seq", "head"),
        check_vma=False,
    )
```

time: 493 us -> 252 us (0.51)
  waiting for transfers between devices: 266 us -> 120 us
  blocking collectives: 100 us -> 18.5 us
  starting transfers between devices: 8.02 us -> 42.9 us
  other arithmetic: 46.1 us -> 12.2 us
  local copies, waits for them, and re-layouts: 25.7 us -> 15.8 us
    all_to_all x1, blocking collectives: 100 us -> 18.5 us  [shards(): lax.all_to_all(outgoing, 'seq', split_axis=0, concat_axis=0, tiled=True)]
    psum x1 -> x0, waiting for transfers between devices: 66.3 us -> none  [shards(): lax.psum(head_term.astype(jnp.bfloat16), 'head').astype(jnp.float32)]
    reduce_scatter x2 -> x0, waiting for transfers between devices: 39.5 us -> none  [the longest x1 39.5 us: shards(): lax.psum_scatter(routed.astype(jnp.float32).astype(jnp.bfloat16), 'head',...]
    all_to_all x1 -> x6, starting transfers between devices: 7.9 us -> 42.6 us  [the longest x2 12.6 us: head_columns(): lax.all_to_all(weights, 'head', split_axis=1, concat_axis=0, tiled=True)]
    select_n x34 -> x0, other arithmetic: 34.6 us -> none  [the longest x32 30.4 us: hop(): return jnp.where(reached, new, before)]
    all_gather x1 -> x4, waiting for transfers between devices: 75.5 us -> 53.7 us  [gather_columns(): return lax.all_gather(block, 'head', axis=1, tiled=True)]
    all_to_all x1 -> x6, waiting for transfers between devices: 84.9 us -> 66.1 us  [the longest x2 23.7 us: head_columns(): lax.all_to_all(weights, 'head', split_axis=1, concat_axis=0, tiled=True)]
    gather x2 -> x0, local copies, waits for them, and re-layouts: 13.2 us -> none  [the longest x1 7.13 us: shards(): jnp.take(returned.reshape(EXPERTS * CAP, returned_width), slot_index, axi...]
  transfers between devices with their start and end apart: 5 -> 10, of which waited for: 4 -> 8; matrix products, arithmetic and copies ran while one was open for 5% -> 9% of each run, Pallas kernels for 0% -> 0%
where the time goes in v1:
time: 252 us; the launch traced here: 248 us
  waiting for transfers between devices  120 us (48%)
  starting transfers between devices  42.9 us (17%)
  matrix products  25.3 us (10%)
  blocking collectives  18.5 us (7%)
  local copies, waits for them, and re-layouts  15.8 us (6%)
  between operations  13.5 us (5%)
  other arithmetic  12.2 us (5%)
    all_gather x4, waiting for transfers between devices, gather_columns(): return lax.all_gather(block, 'head', axis=1, tiled=True)  53.7 us
    all_to_all x2, waiting for transfers between devices, head_columns(): lax.all_to_all(weights, 'head', split_axis=1, concat_axis=0, tiled=True)  23.7 us
    all_to_all x1, blocking collectives, shards(): lax.all_to_all(outgoing, 'seq', split_axis=0, concat_axis=0, tiled=True)  18.5 us
    all_to_all x1, waiting for transfers between devices, shards(): lax.all_to_all(expert_down, 'head', split_axis=2, concat_axis=1, tiled=True)  17.8 us
    all_to_all x1, waiting for transfers between devices, shards(): lax.all_to_all(routed_out, 'seq', split_axis=0, concat_axis=0, tiled=True)  12.7 us
    all_to_all x2, starting transfers between devices, head_columns(): lax.all_to_all(weights, 'head', split_axis=1, concat_axis=0, tiled=True)  12.6 us
    dot_general x8, matrix products, dot(): return jnp.dot(a, b, preferred_element_type=F32)  12.4 us
    all_to_all x1, starting transfers between devices, carried_state(): lax.all_to_all(chunks, 'seq', split_axis=0, concat_axis=0, tiled=True)  12 us
  transfers between devices with their start and end apart: 10, of which 8 were waited for; matrix products, arithmetic and copies ran while one was open for 9% of the time, Pallas kernels for 0%

profile of v1, /device:TPU:1, one launch (start us, length us, event | category | flops | bytes accessed | tf_op | source)
XLA Modules:
  0.0 248.1 jit_solution(1890059835473310391)
XLA Ops:
  6.5 2.2 fusion
  12.1 12.0 %all-to-all-start = ((f32[32,8,128]{2,1,0:T(8,128)}), f32[32,8,128]{2,1,0:T(8,128)S(1)}, u32[]{:S(2)}, u32[]{:S(2)}) async-start(f32[32,8,128]{2,1,0:T(8,128)} %bitcast.3), calls=%async_computation | async-start | bytes 262144 | tf_op jit(solution)/shard_map/all_to_all | solution.py:34
  25.0 2.1 convolution_convert_fusion.2
  28.3 5.0 %all-to-all-done = f32[32,8,128]{2,1,0:T(8,128)S(1)} async-done(((f32[32,8,128]{2,1,0:T(8,128)}), f32[32,8,128]{2,1,0:T(8,128)S(1)}, u32[]{:S(2)}, u32[]{:S(2)}) %all-to-all-start) | async-done | bytes 131104 | tf_op jit(solution)/shard_map/all_to_all | solution.py:34
  33.3 2.1 select_reduce_fusion
  35.4 4.2 %all-to-all-start.1 = ((f32[32,8,128]{2,1,0:T(8,128)}), f32[32,8,128]{2,1,0:T(8,128)S(1)}, u32[]{:S(2)}, u32[]{:S(2)}) async-start(f32[32,8,128]{2,1,0:T(8,128)} %select_reduce_fusion), calls=%async_computation.1 | async-start | bytes 262144 | tf_op jit(solution)/shard_map/all_to_all | solution.py:37
  39.7 2.3 fusion.4
  41.9 6.8 %all-to-all-done.1 = f32[32,8,128]{2,1,0:T(8,128)S(1)} async-done(((f32[32,8,128]{2,1,0:T(8,128)}), f32[32,8,128]{2,1,0:T(8,128)S(1)}, u32[]{:S(2)}, u32[]{:S(2)}) %all-to-all-start.1) | async-done | bytes 131104 | tf_op jit(solution)/shard_map/all_to_all | solution.py:37
  50.4 1.2 fusion.22
  54.2 2.3 copy.65
  56.5 7.3 %all-to-all-start.2 = ((bf16[256,8,256]{0,2,1:T(8,128)(2,1)}), bf16[256,8,256]{0,2,1:T(8,128)(2,1)S(1)}, u32[]{:S(2)}, u32[]{:S(2)}) async-start(bf16[256,8,256]{0,2,1:T(8,128)(2,1)} %bitcast.7), calls=%async_computation.2 | async-start | bytes 2097152 | tf_op jit(solution)/shard_map/all_to_all | solution.py:23
  63.8 23.7 %all-to-all-done.2 = bf16[256,8,256]{0,2,1:T(8,128)(2,1)S(1)} async-done(((bf16[256,8,256]{0,2,1:T(8,128)(2,1)}), bf16[256,8,256]{0,2,1:T(8,128)(2,1)S(1)}, u32[]{:S(2)}, u32[]{:S(2)}) %all-to-all-start.2) | async-done | bytes 1048608 | tf_op jit(solution)/shard_map/all_to_all | solution.py:23
  88.0 3.2 %fusion.29 = (bf16[512,256]{1,0:T(8,128)(2,1)}, f32[512,256]{1,0:T(8,128)}) fusion(bf16[512,2048]{0,1:T(8,128)(2,1)} %all-gather.5.cloned.1.call-done, bf16[2048,256]{1,0:T(8,128)(2,1)S(1)} %bitcast.73, bf16[512,2048]{1,0:T(8,128)(2,1)} %param.12, s32[]{:T(128)S(6)} %select_n.11), kind=kOutput, calls=%fused_computation.59 | convolution fusion | flops 537264128 | bytes 4194308 | tf_op jit(solution)/shard_map/dot_general | solution.py:14
  91.6 1.4 fusion.5
  93.0 18.5 %all_to_all.76 = bf16[32,2,16,256]{3,2,1,0:T(8,128)(2,1)S(1)} all-to-all(bf16[32,2,16,256]{3,2,1,0:T(8,128)(2,1)S(1)} %bitcast.77), channel_id=1, replica_groups=mesh['seq'=32,'head'=8] {'seq'}, dimensions={0} | all-to-all | bytes 1048576 | tf_op jit(solution)/shard_map/all_to_all | solution.py:103
  112.6 3.9 %all-gather.7.cloned.1.call-done = bf16[512,2048]{1,0:T(8,128)(2,1)} async-done(((bf16[512,256]{1,0:T(8,128)(2,1)}), bf16[512,2048]{1,0:T(8,128)(2,1)}) %all-gather.7.cloned.1.call-update) | async-done | bytes 2097168 | tf_op jit(solution)/shard_map/all_gather | solution.py:27
  116.5 2.2 multiply_reduce_fusion.1
  120.2 37.2 %all-gather.9.cloned.1.call-done = bf16[1024,2048]{1,0:T(8,128)(2,1)} async-done(((bf16[1024,256]{1,0:T(8,128)(2,1)}), bf16[1024,2048]{1,0:T(8,128)(2,1)}) %all-gather.9.cloned.1.call-update) | async-done | bytes 4194320 | tf_op jit(solution)/shard_map/all_gather | solution.py:27
  157.3 3.1 %multiply_reduce_fusion = f32[1024]{0:T(1024)S(1)} fusion(bf16[1024,2048]{1,0:T(8,128)(2,1)} %all-gather.9.cloned.1.call-done), kind=kLoop, calls=%fused_computation | loop fusion | flops 6290432 | bytes 4198400 | tf_op jit(solution)/shard_map/reduce_sum | solution.py:43
  160.5 3.6 %convolution_multiply_fusion.1 = f32[2,512,128]{2,1,0:T(8,128)S(1)} fusion(bf16[2,512,2048]{2,1,0:T(8,128)(2,1)} %bitcast.57, bf16[2,2048,128]{2,1,0:T(8,128)(2,1)S(1)} %copy-done.11, f32[2,512]{1,0:T(2,128)S(1)} %rsqrt.40), kind=kOutput, calls=%fused_computation.23 | convolution fusion | flops 537001984 | bytes 5771264 | tf_op jit(solution)/shard_map/erd,edf->erf/dot_general | solution.py:115
  164.2 1.3 fusion.10
  166.3 2.0 copy.70
  168.3 4.2 %all-to-all-start.5 = ((bf16[2,128,2048]{1,0,2:T(2,128)(2,1)}), bf16[2,128,2048]{1,0,2:T(2,128)(2,1)S(1)}, u32[]{:S(2)}, u32[]{:S(2)}) async-start(bf16[2,128,2048]{1,0,2:T(2,128)(2,1)} %copy.70), calls=%async_computation.5 | async-start | bytes 2097152 | tf_op jit(solution)/shard_map/all_to_all | solution.py:70
  173.6 17.8 %all-to-all-done.5 = bf16[2,128,2048]{1,0,2:T(2,128)(2,1)S(1)} async-done(((bf16[2,128,2048]{1,0,2:T(2,128)(2,1)}), bf16[2,128,2048]{1,0,2:T(2,128)(2,1)S(1)}, u32[]{:S(2)}, u32[]{:S(2)}) %all-to-all-start.5) | async-done | bytes 1048608 | tf_op jit(solution)/shard_map/all_to_all | solution.py:70
  191.4 5.3 %all-to-all-start.4 = ((bf16[128,8,256]{0,2,1:T(8,128)(2,1)}), bf16[128,8,256]{0,2,1:T(8,128)(2,1)}, u32[]{:S(2)}, u32[]{:S(2)}) async-start(bf16[128,8,256]{0,2,1:T(8,128)(2,1)} %bitcast.16), calls=%async_computation.4 | async-start | bytes 1048576 | tf_op jit(solution)/shard_map/all_to_all | solution.py:23
  196.7 2.0 copy.71
  198.7 12.7 %all-gather.11.cloned.1.call-done = bf16[1536,1024]{1,0:T(8,128)(2,1)} async-done(((bf16[1536,128]{1,0:T(8,128)(2,1)}), bf16[1536,1024]{1,0:T(8,128)(2,1)}) %all-gather.11.cloned.1.call-update) | async-done | bytes 3145744 | tf_op jit(solution)/shard_map/all_gather | solution.py:27
  211.4 1.6 slice-done
  214.8 9.6 %all-to-all-start.6 = ((bf16[32,2,16,256]{3,2,1,0:T(8,128)(2,1)}), bf16[32,2,16,256]{3,2,1,0:T(8,128)(2,1)S(1)}, u32[]{:S(2)}, u32[]{:S(2)}) async-start(bf16[32,2,16,256]{3,2,1,0:T(8,128)(2,1)} %bitcast.56), calls=%async_computation.6 | async-start | bytes 1048576 | tf_op jit(solution)/shard_map/all_to_all | solution.py:128
  224.4 1.2 copy.69
  225.7 12.7 %all-to-all-done.6 = bf16[32,2,16,256]{3,2,1,0:T(8,128)(2,1)S(1)} async-done(((bf16[32,2,16,256]{3,2,1,0:T(8,128)(2,1)}), bf16[32,2,16,256]{3,2,1,0:T(8,128)(2,1)S(1)}, u32[]{:S(2)}, u32[]{:S(2)}) %all-to-all-start.6) | async-done | bytes 524320 | tf_op jit(solution)/shard_map/all_to_all | solution.py:128
  239.2 2.4 fusion.11
  (77 shorter events, 17.5 us)
Async XLA Ops:
  6.5 2.2 copy-start
  6.5 2.5 %copy-start.5 = (bf16[512,2048]{1,0:T(8,128)(2,1)S(1)}, bf16[512,2048]{1,0:T(8,128)(2,1)}, u32[]{:S(2)}) copy-start(bf16[512,2048]{1,0:T(8,128)(2,1)} %param.12) | copy-start | bytes 6291460
  9.1 1.2 copy-start.17
  10.3 0.9 copy-start.7
  12.1 21.2 %all-to-all-start = ((f32[32,8,128]{2,1,0:T(8,128)}), f32[32,8,128]{2,1,0:T(8,128)S(1)}, u32[]{:S(2)}, u32[]{:S(2)}) async-start(f32[32,8,128]{2,1,0:T(8,128)} %bitcast.3), calls=%async_computation | async-start | bytes 262144 | tf_op jit(solution)/shard_map/all_to_all | solution.py:34
  25.0 2.8 %copy-start.8 = (bf16[512,256]{0,1:T(8,128)(2,1)S(1)}, bf16[512,256]{0,1:T(8,128)(2,1)}, u32[]{:S(2)}) copy-start(bf16[512,256]{0,1:T(8,128)(2,1)} %copy-done.7) | copy-start | bytes 786436
  27.1 0.7 copy-start.4
  35.4 13.4 %all-to-all-start.1 = ((f32[32,8,128]{2,1,0:T(8,128)}), f32[32,8,128]{2,1,0:T(8,128)S(1)}, u32[]{:S(2)}, u32[]{:S(2)}) async-start(f32[32,8,128]{2,1,0:T(8,128)} %select_reduce_fusion), calls=%async_computation.1 | async-start | bytes 262144 | tf_op jit(solution)/shard_map/all_to_all | solution.py:37
  39.6 48.4 %all-gather.5.cloned.1.call-start = ((), (), s32[]{:S(2)}) async-start(), calls=%async_computation.7 | async-start | bytes 2359296 | tf_op jit(solution)/shard_map/all_gather | solution.py:27
  48.8 0.7 copy-start.14
  50.4 2.4 copy-start.3
  50.4 2.4 copy-start.6
  56.5 31.0 %all-to-all-start.2 = ((bf16[256,8,256]{0,2,1:T(8,128)(2,1)}), bf16[256,8,256]{0,2,1:T(8,128)(2,1)S(1)}, u32[]{:S(2)}, u32[]{:S(2)}) async-start(bf16[256,8,256]{0,2,1:T(8,128)(2,1)} %bitcast.7), calls=%async_computation.2 | async-start | bytes 2097152 | tf_op jit(solution)/shard_map/all_to_all | solution.py:23
  63.8 52.7 %all-gather.7.cloned.1.call-start = ((), (), s32[]{:S(2)}) async-start(), calls=%async_computation.8 | async-start | bytes 2359296 | tf_op jit(solution)/shard_map/all_gather | solution.py:27
  88.0 3.3 %copy-start.16 = (s32[512,1]{0,1:T(1,128)S(1)}, s32[512,1]{0,1:T(1,128)}, u32[]{:S(2)}) copy-start(s32[512,1]{0,1:T(1,128)} %param.23) | copy-start | bytes 6148
  91.3 66.1 %all-gather.9.cloned.1.call-start = ((), (), s32[]{:S(2)}) async-start(), calls=%async_computation.9 | async-start | bytes 4718592 | tf_op jit(solution)/shard_map/all_gather | solution.py:27
  111.5 7.2 %copy-start.12 = (bf16[2048,128]{1,0:T(8,128)(2,1)S(1)}, bf16[2048,128]{1,0:T(8,128)(2,1)}, u32[]{:S(2)}) copy-start(bf16[2048,128]{1,0:T(8,128)(2,1)} %param.17) | copy-start | bytes 1572868
  112.3 7.1 %copy-start.19 = (bf16[2048,128]{1,0:T(8,128)(2,1)S(1)}, bf16[2048,128]{1,0:T(8,128)(2,1)}, u32[]{:S(2)}) copy-start(bf16[2048,128]{1,0:T(8,128)(2,1)} %param.18) | copy-start | bytes 1572868
  112.3 99.0 %all-gather.11.cloned.1.call-start = ((), (), s32[]{:S(2)}) async-start(), calls=%async_computation.10 | async-start | bytes 3538944 | tf_op jit(solution)/shard_map/all_gather | solution.py:27
  116.5 2.2 copy-start.2
  120.2 40.3 %copy-start.11 = (bf16[2,2048,128]{2,1,0:T(8,128)(2,1)S(1)}, bf16[2,2048,128]{2,1,0:T(8,128)(2,1)}, u32[]{:S(2)}) copy-start(bf16[2,2048,128]{2,1,0:T(8,128)(2,1)} %param.20) | copy-start | bytes 3145732
  160.4 3.6 %copy-start.1 = (bf16[1024,2048]{1,0:T(8,128)(2,1)S(1)}, bf16[1024,2048]{1,0:T(8,128)(2,1)}, u32[]{:S(2)}) copy-start(bf16[1024,2048]{1,0:T(8,128)(2,1)} %all-gather.9.cloned.1.call-done) | copy-start | bytes 12582916
  160.5 3.7 %copy-start.18 = (bf16[2,2048,128]{2,1,0:T(8,128)(2,1)S(1)}, bf16[2,2048,128]{2,1,0:T(8,128)(2,1)}, u32[]{:S(2)}) copy-start(bf16[2,2048,128]{2,1,0:T(8,128)(2,1)} %param.21) | copy-start | bytes 3145732
  164.2 2.1 copy-start.9
  166.3 6.3 %copy-start.13 = (bf16[128,2048]{1,0:T(8,128)(2,1)S(1)}, bf16[128,2048]{1,0:T(8,128)(2,1)}, u32[]{:S(2)}) copy-start(bf16[128,2048]{1,0:T(8,128)(2,1)} %param.19) | copy-start | bytes 1572868
  168.3 23.1 %all-to-all-start.5 = ((bf16[2,128,2048]{1,0,2:T(2,128)(2,1)}), bf16[2,128,2048]{1,0,2:T(2,128)(2,1)S(1)}, u32[]{:S(2)}, u32[]{:S(2)}) async-start(bf16[2,128,2048]{1,0,2:T(2,128)(2,1)} %copy.70), calls=%async_computation.5 | async-start | bytes 2097152 | tf_op jit(solution)/shard_map/all_to_all | solution.py:70
  191.4 23.4 %all-to-all-start.4 = ((bf16[128,8,256]{0,2,1:T(8,128)(2,1)}), bf16[128,8,256]{0,2,1:T(8,128)(2,1)}, u32[]{:S(2)}, u32[]{:S(2)}) async-start(bf16[128,8,256]{0,2,1:T(8,128)(2,1)} %bitcast.16), calls=%async_computation.4 | async-start | bytes 1048576 | tf_op jit(solution)/shard_map/all_to_all | solution.py:23
  211.4 1.6 slice-start
  211.4 1.9 copy-start.10
  214.8 24.3 %copy-start.15 = (f32[512,256]{1,0:T(8,128)S(1)}, f32[512,256]{1,0:T(8,128)}, u32[]{:S(2)}) copy-start(f32[512,256]{1,0:T(8,128)} %get-tuple-element.8) | copy-start | bytes 1572868
  214.8 23.6 %all-to-all-start.6 = ((bf16[32,2,16,256]{3,2,1,0:T(8,128)(2,1)}), bf16[32,2,16,256]{3,2,1,0:T(8,128)(2,1)S(1)}, u32[]{:S(2)}, u32[]{:S(2)}) async-start(bf16[32,2,16,256]{3,2,1,0:T(8,128)(2,1)} %bitcast.56), calls=%async_computation.6 | async-start | bytes 1048576 | tf_op jit(solution)/shard_map/all_to_all | solution.py:128
Sparse Core Ops, SparseCore 0:
  54.4 31.7 all-gather.4
  91.4 25.0 all-gather.6
  118.3 39.0 all-gather.8
  166.4 44.9 all-gather.10

commit v2 on v1

v2 whole, which is shorter than its diff:
```python
import functools

import jax
import jax.numpy as jnp
from jax import lax
from jax.experimental import pallas as pl
from jax.experimental.pallas import tpu as pltpu
from jax.sharding import PartitionSpec as P

HD = 128
CAP = 16
F32 = jnp.float32
BF16 = jnp.bfloat16

STATE, CARRY, DISPATCH, RETURN = range(4)
HEADS, MIDDLE, ROUTED, SHARED_HIDDEN, ROUTED_HIDDEN = 0, 1, 2, 4, 5
GATHERS = 7


def dot(a, b, contract=((1,), (0,))):
    return lax.dot_general(a, b, (contract, ((), ())), preferred_element_type=F32)


def two_part(values):
    high = values.astype(BF16)
    return high, (values - high.astype(F32)).astype(BF16)


def rms(total, count):
    return lax.rsqrt(total * (1.0 / count) + 1e-06)


def silu(v):
    return v / (1.0 + jnp.exp(-v))


def layer_kernel(
    n_seq, n_head,
    tok, wq, wk, wv, wo, sg, su, sd, eg, eu, ed, ids_col, ids_row,
    out,
    x, own, normed, wqkv, wo_v, sd_v, ed_v, sgu, egu, qkv, st, got, pre, car, att,
    hn, mid, rin, outb, hs, hr, rout, back, res, chosen, chosen_t, acc, sq,
    load_sem, w_send, w_recv, s_send, s_recv, g_send, g_recv,
):
    rows, width = x.shape
    cols = width // n_head
    owned = eg.shape[0]
    hidden = eg.shape[2]
    span = 2 * HD
    per = n_seq // 2
    s = lax.axis_index("seq")
    h = lax.axis_index("head")
    core = h % 2
    chip = h // 2
    chips = n_head // 2
    partner = 2 * chip + 1 - core
    right = 2 * ((chip + 1) % chips) + core
    left = 2 * ((chip + chips - 1) % chips) + core
    far = 2 * ((chip + 2) % chips) + core

    def twin(b):
        return 2 * (b // 2) + 1 - b % 2

    def col_slice(index, size):
        return pl.ds(pl.multiple_of(index * size, 128), size)

    def load(i, src, dst):
        return pltpu.make_async_copy(src, dst, load_sem.at[i])

    loads = [
        load(0, tok, x),
        load(1, wq, wqkv.at[:, pl.ds(0, span)]),
        load(2, wk, wqkv.at[:, pl.ds(span, span)]),
        load(3, wv, wqkv.at[:, pl.ds(2 * span, span)]),
        load(4, tok.at[:, col_slice(h, cols)], own),
        load(5, wo.at[:, col_slice(h, cols)], wo_v.at[h]),
        load(6, sd.at[:, col_slice(h, cols)], sd_v.at[h]),
        load(7, ed.at[:, :, col_slice(h, cols)], ed_v.at[h]),
        load(8, sg, sgu.at[:, pl.ds(0, hidden)]),
        load(9, su, sgu.at[:, pl.ds(hidden, hidden)]),
        load(10, eg, egu.at[:, :, pl.ds(0, hidden)]),
        load(11, eu, egu.at[:, :, pl.ds(hidden, hidden)]),
    ]

    def seq_peer(t):
        return (s + t) % n_seq

    def head_peer(t):
        return (h + t) % n_head

    barrier = pltpu.get_barrier_semaphore()

    def greet_seq(t, carry):
        pl.semaphore_signal(barrier, inc=1, device_id={"seq": seq_peer(t)})
        return carry

    def greet_head(t, carry):
        pl.semaphore_signal(barrier, inc=1, device_id={"head": head_peer(t)})
        return carry

    lax.fori_loop(1, n_head, greet_head, 0)
    lax.fori_loop(1, n_seq, greet_seq, 0)
    for copy in loads:
        copy.start()

    def weight_copy(i, peer):
        src, dst = (
            (wo.at[:, col_slice(peer, cols)], wo_v.at[h]),
            (sd.at[:, col_slice(peer, cols)], sd_v.at[h]),
            (ed.at[:, :, col_slice(peer, cols)], ed_v.at[h]),
        )[i]
        return pltpu.make_async_remote_copy(
            src, dst, w_send.at[i, peer], w_recv.at[i, h], device_id={"head": peer}
        )

    def weight_arrival(i, source):
        dst = (wo_v, sd_v, ed_v)[i].at[source]
        return pltpu.make_async_remote_copy(
            dst, dst, w_send.at[i, source], w_recv.at[i, source], device_id={"head": source}
        )

    def seq_copy(e, peer):
        src, dst = (
            (st.at[peer], got.at[s]),
            (pre.at[peer], car.at[s]),
            (outb.at[peer], rin.at[h, :, s]),
            (rout.at[:, peer], back.at[s]),
        )[e]
        return pltpu.make_async_remote_copy(
            src, dst, s_send.at[e, peer], s_recv.at[e, s], device_id={"seq": peer}
        )

    def seq_arrival(e, source):
        dst = (got.at[source], car.at[source], rin.at[h, :, source], back.at[source])[e]
        return pltpu.make_async_remote_copy(
            dst, dst, s_send.at[e, source], s_recv.at[e, source], device_id={"seq": source}
        )

    def seq_start(e):
        def one(t, carry):
            seq_copy(e, seq_peer(t)).start()
            return carry

        lax.fori_loop(1, n_seq, one, 0)

    def seq_wait(e):
        def one(t, carry):
            seq_arrival(e, seq_peer(t)).wait_recv()
            return carry

        lax.fori_loop(1, n_seq, one, 0)

    def view(g, b):
        if g == HEADS:
            return hn.at[b]
        if g == MIDDLE:
            return mid.at[b]
        if g == SHARED_HIDDEN:
            return hs.at[b]
        if g >= ROUTED_HIDDEN:
            return hr.at[b, g - ROUTED_HIDDEN]
        return rin.at[b, g - ROUTED]

    def half(g, b, k):
        whole = view(g, b)
        n = whole.shape[0] // 2
        return whole.at[pl.ds(k * n, n)]

    def leg(g, i):
        ref, target = (
            (lambda: view(g, h), right),
            (lambda: view(g, h), left),
            (lambda: view(g, h), partner),
            (lambda: half(g, left, 0), right),
            (lambda: half(g, right, 1), left),
            (lambda: view(g, left), partner),
            (lambda: view(g, right), partner),
            (lambda: half(g, far, 0), partner),
            (lambda: half(g, far, 1), partner),
        )[i]
        ref = ref()
        return pltpu.make_async_remote_copy(
            ref, ref, g_send.at[g, i], g_recv.at[g, i], device_id={"head": target}
        )

    def leg_wait(g, i):
        ref = (
            lambda: view(g, left),
            lambda: view(g, right),
            lambda: view(g, partner),
            lambda: half(g, far, 0),
            lambda: half(g, far, 1),
            lambda: view(g, twin(left)),
            lambda: view(g, twin(right)),
            lambda: half(g, twin(far), 0),
            lambda: half(g, twin(far), 1),
        )[i]()
        pltpu.make_async_remote_copy(
            ref, ref, g_send.at[g, i], g_recv.at[g, i], device_id={"head": partner}
        ).wait_recv()

    def gather_start(g):
        for i in range(3):
            leg(g, i).start()

    def gather_pass(g):
        leg_wait(g, 0)
        leg(g, 3).start()
        leg(g, 5).start()
        leg_wait(g, 1)
        leg(g, 4).start()
        leg(g, 6).start()

    def gather_far(g):
        leg_wait(g, 3)
        leg(g, 7).start()
        leg_wait(g, 4)
        leg(g, 8).start()

    def gather_use(g, use):
        use(h)
        leg_wait(g, 2)
        use(partner)
        gather_pass(g)
        use(left)
        use(right)
        gather_far(g)
        leg_wait(g, 5)
        use(twin(left))
        leg_wait(g, 6)
        use(twin(right))
        use(far)
        leg_wait(g, 7)
        leg_wait(g, 8)
        use(twin(far))

    loads[0].wait()

    def normalize(i, carry):
        at = pl.ds(pl.multiple_of(i * 32, 32), 32)
        wide = x[at, :].astype(F32)
        scale = rms(jnp.sum(wide * wide, axis=-1, keepdims=True), width)
        normed[at, :] = (wide * scale).astype(BF16)
        return carry

    lax.fori_loop(0, rows // 32, normalize, 0)
    pl.semaphore_wait(barrier, n_head - 1 + n_seq - 1)

    for i in range(3):

        def one(t, carry):
            weight_copy(i, head_peer(t)).start()
            return carry

        lax.fori_loop(1, n_head, one, 0)
    for i in (1, 2, 3):
        loads[i].wait()
    block = min(256, rows)

    def project(i, carry):
        at = pl.ds(pl.multiple_of(i * block, block), block)
        qkv[at, :] = dot(normed[at, :], wqkv[...]).astype(BF16)
        return carry

    lax.fori_loop(0, rows // block, project, 0)

    for a in range(2):
        k = qkv[:, span + a * HD : span + (a + 1) * HD]
        v = qkv[:, 2 * span + a * HD : 2 * span + (a + 1) * HD]
        st[a * per : (a + 1) * per] = dot(k, v, ((0,), (0,))).reshape(per, -1, HD)
    seq_start(STATE)
    got[s] = st[s]

    for a in range(2):
        for i in range(rows // block):
            top, end = i * block, (i + 1) * block
            q = qkv[top:end, a * HD : (a + 1) * HD]
            k = qkv[:end, span + a * HD : span + (a + 1) * HD]
            v = qkv[:end, 2 * span + a * HD : 2 * span + (a + 1) * HD]
            scores = dot(q, k, ((1,), (1,)))
            row = lax.broadcasted_iota(jnp.int32, scores.shape, 0) + top
            col = lax.broadcasted_iota(jnp.int32, scores.shape, 1)
            high, low = two_part(jnp.where(row >= col, scores, 0.0))
            att[top:end, a * HD : (a + 1) * HD] = dot(high, v) + dot(low, v)

    def running(j, total):
        @pl.when(j != s)
        def _():
            seq_arrival(STATE, j).wait_recv()

        pre[j] = total
        return total + got[j]

    lax.fori_loop(0, n_seq, running, jnp.zeros(pre.shape[1:], F32))
    seq_start(CARRY)
    car[s] = pre[s]

    ids_c = ids_col[...]
    ids_r = ids_row[...]
    row = lax.broadcasted_iota(jnp.int32, (rows, rows), 0)
    col = lax.broadcasted_iota(jnp.int32, (rows, rows), 1)
    same = ids_c == ids_r
    rank_r = jnp.sum(jnp.where(same & (row <= col), 1.0, 0.0), axis=0, keepdims=True)
    rank_c = jnp.sum(jnp.where(same & (col <= row), 1.0, 0.0), axis=1, keepdims=True)
    base_r = ids_r.astype(F32) * CAP + rank_r - 1.0
    base_c = ids_c.astype(F32) * CAP + rank_c - 1.0
    slots = n_seq * owned * CAP
    place = lax.broadcasted_iota(jnp.int32, (slots, 1), 0).astype(F32)
    chosen[...] = jnp.where(place == base_r, 1.0, 0.0).astype(BF16)
    place = lax.broadcasted_iota(jnp.int32, (1, slots), 1).astype(F32)
    chosen_t[...] = jnp.where(place == base_c, 1.0, 0.0).astype(BF16)

    seq_wait(CARRY)
    for a in range(2):
        high, low = two_part(car[a * per : (a + 1) * per].reshape(HD, HD))
        q = qkv[:, a * HD : (a + 1) * HD]
        whole = att[:, a * HD : (a + 1) * HD] + dot(q, high) + dot(q, low)
        scale = rms(jnp.sum(whole * whole, axis=-1, keepdims=True), HD)
        hn[h, :, a * HD : (a + 1) * HD] = (whole * scale).astype(BF16)
    gather_start(HEADS)

    loads[4].wait()
    res[...] = own[...].astype(F32)
    loads[5].wait()

    def weights_wait(i):
        def one(t, carry):
            weight_arrival(i, head_peer(t)).wait_recv()
            return carry

        lax.fori_loop(1, n_head, one, 0)

    weights_wait(0)

    def use_heads(b):
        res[...] += dot(hn[b], wo_v[b])

    gather_use(HEADS, use_heads)
    mid[h] = res[...].astype(BF16)
    gather_start(MIDDLE)
    outb[...] = dot(chosen[...], mid[h]).astype(BF16).reshape(outb.shape)
    seq_start(DISPATCH)
    rin[h, :, s] = outb[s]

    loads[8].wait()
    loads[9].wait()
    acc[...] = jnp.zeros_like(acc)
    sq[...] = jnp.zeros_like(sq)

    def use_middle(b):
        part = mid[b]
        acc[pl.ds(0, rows), :] += dot(part, sgu[pl.ds(pl.multiple_of(b * cols, cols), cols), :])
        wide = part.astype(F32)
        sq[pl.ds(0, rows), :] += wide * wide

    def activate(count):
        scale = rms(jnp.sum(sq[pl.ds(0, count), :], axis=-1, keepdims=True), width)
        gate = acc[pl.ds(0, count), pl.ds(0, hidden)] * scale
        up = acc[pl.ds(0, count), pl.ds(hidden, hidden)] * scale
        return (silu(gate) * up).astype(BF16)

    gather_use(MIDDLE, use_middle)

    seq_wait(DISPATCH)
    for e in range(owned):
        gather_start(ROUTED + e)
    hs[h] = activate(rows)
    gather_start(SHARED_HIDDEN)
    loads[10].wait()
    loads[11].wait()
    taken = n_seq * CAP
    for e in range(owned):
        acc[...] = jnp.zeros_like(acc)
        sq[...] = jnp.zeros_like(sq)

        def use_routed(b):
            part = rin[b, e].reshape(taken, cols)
            acc[pl.ds(0, taken), :] += dot(part, egu[e, pl.ds(pl.multiple_of(b * cols, cols), cols), :])
            wide = part.astype(F32)
            sq[pl.ds(0, taken), :] += wide * wide

        gather_use(ROUTED + e, use_routed)
        hr[h, e] = activate(taken)
        gather_start(ROUTED_HIDDEN + e)

    loads[6].wait()
    loads[7].wait()
    weights_wait(1)
    weights_wait(2)

    def use_shared(b):
        res[...] += dot(hs[b], sd_v[b])

    gather_use(SHARED_HIDDEN, use_shared)
    for e in range(owned):
        acc[...] = jnp.zeros_like(acc)

        def use_hidden(b):
            acc[pl.ds(0, taken), pl.ds(0, cols)] += dot(hr[b, e], ed_v[b, e])

        gather_use(ROUTED_HIDDEN + e, use_hidden)
        rout[e] = acc[pl.ds(0, taken), pl.ds(0, cols)].astype(BF16).reshape(rout.shape[1:])
    seq_start(RETURN)
    back[s] = rout[:, s]
    seq_wait(RETURN)
    routed = dot(chosen_t[...], back[...].reshape(slots, cols))
    out[...] = (res[...] + routed).astype(BF16)

    def weights_left(t, carry):
        for i in range(3):
            weight_copy(i, head_peer(t)).wait_send()
        return carry

    lax.fori_loop(1, n_head, weights_left, 0)

    def seq_left(t, carry):
        for e in range(4):
            seq_copy(e, seq_peer(t)).wait_send()
        return carry

    lax.fori_loop(1, n_seq, seq_left, 0)
    for g in range(GATHERS):
        for i in range(9):
            leg(g, i).wait_send()


def shards(
    tokens,
    w_query,
    w_key,
    w_value,
    w_out,
    shared_gate,
    shared_up,
    shared_down,
    expert_gate,
    expert_up,
    expert_down,
    expert_ids,
):
    n_seq, n_head = lax.axis_size("seq"), lax.axis_size("head")
    rows, width = tokens.shape
    cols = width // n_head
    owned, _, hidden = expert_gate.shape
    heads = w_query.shape[1]
    taken = n_seq * CAP
    slots = owned * taken
    chunk = heads // n_seq
    most = max(rows, taken)
    any_spec = pl.BlockSpec(memory_space=pl.ANY)
    vmem_spec = pl.BlockSpec(memory_space=pltpu.VMEM)
    V = pltpu.VMEM
    dma = pltpu.SemaphoreType.DMA
    return pl.pallas_call(
        functools.partial(layer_kernel, n_seq, n_head),
        out_shape=jax.ShapeDtypeStruct((rows, cols), BF16),
        in_specs=[any_spec] * 11 + [vmem_spec] * 2,
        out_specs=vmem_spec,
        scratch_shapes=[
            V((rows, width), BF16),
            V((rows, cols), BF16),
            V((rows, width), BF16),
            V((width, 3 * heads), BF16),
            V((n_head, heads, cols), BF16),
            V((n_head, hidden, cols), BF16),
            V((n_head, owned, hidden, cols), BF16),
            V((width, 2 * hidden), BF16),
            V((owned, width, 2 * hidden), BF16),
            V((rows, 3 * heads), BF16),
            V((n_seq, chunk, HD), F32),
            V((n_seq, chunk, HD), F32),
            V((n_seq, chunk, HD), F32),
            V((n_seq, chunk, HD), F32),
            V((rows, heads), F32),
            V((n_head, rows, heads), BF16),
            V((n_head, rows, cols), BF16),
            V((n_head, owned, n_seq, CAP, cols), BF16),
            V((n_seq, owned, CAP, cols), BF16),
            V((n_head, rows, hidden), BF16),
            V((n_head, owned, taken, hidden), BF16),
            V((owned, n_seq, CAP, cols), BF16),
            V((n_seq, owned, CAP, cols), BF16),
            V((rows, cols), F32),
            V((slots, rows), BF16),
            V((rows, slots), BF16),
            V((most, 2 * hidden), F32),
            V((most, cols), F32),
            dma((12,)),
            dma((3, n_head)),
            dma((3, n_head)),
            dma((4, n_seq)),
            dma((4, n_seq)),
            dma((GATHERS, 9)),
            dma((GATHERS, 9)),
        ],
        compiler_params=pltpu.CompilerParams(
            collective_id=0, has_side_effects=True, vmem_limit_bytes=60 * 1024 * 1024
        ),
    )(
        tokens, w_query, w_key, w_value, w_out, shared_gate, shared_up, shared_down,
        expert_gate, expert_up, expert_down, expert_ids, expert_ids.reshape(1, rows),
    )


def solution(mesh):
    return jax.shard_map(
        shards,
        mesh=mesh,
        in_specs=(
            P("seq", None),
            P(None, "head"),
            P(None, "head"),
            P(None, "head"),
            P("head", None),
            P(None, "head"),
            P(None, "head"),
            P("head", None),
            P("seq", None, "head"),
            P("seq", None, "head"),
            P("seq", "head", None),
            P("seq", None),
        ),
        out_specs=P("seq", "head"),
        check_vma=False,
    )
```

time: 252 us -> 144 us (0.57); the launches traced: 248 us -> 144 us
  Pallas kernels: 0 us -> 140 us
  waiting for transfers between devices: 120 us -> 0 us
  starting transfers between devices: 42.9 us -> 0 us
  matrix products: 25.3 us -> 0 us
  blocking collectives: 18.5 us -> 0 us
  between operations: 13.5 us -> 0.01 us
  local copies, waits for them, and re-layouts: 15.8 us -> 3.2 us
  other arithmetic: 12.2 us -> 0 us
    pallas_call x0 -> x1, Pallas kernels: none -> 140 us  [shards(): pl.pallas_call(functools.partial(layer_kernel, n_seq, n_head), out_shape=...]
    all_to_all x6 -> x0, waiting for transfers between devices: 66.1 us -> none  [the longest x2 23.7 us: head_columns(): lax.all_to_all(weights, 'head', split_axis=1, concat_axis=0, tiled=True)]
    all_gather x4 -> x0, waiting for transfers between devices: 53.7 us -> none  [gather_columns(): return lax.all_gather(block, 'head', axis=1, tiled=True)]
    all_to_all x6 -> x0, starting transfers between devices: 42.6 us -> none  [the longest x2 12.6 us: head_columns(): lax.all_to_all(weights, 'head', split_axis=1, concat_axis=0, tiled=True)]
    dot_general x18 -> x0, matrix products: 25.3 us -> none  [the longest x8 12.4 us: dot(): return jnp.dot(a, b, preferred_element_type=F32)]
    all_to_all x1 -> x0, blocking collectives: 18.5 us -> none  [shards(): lax.all_to_all(outgoing, 'seq', split_axis=0, concat_axis=0, tiled=True)]
    reduce_sum x5 -> x0, other arithmetic: 9.82 us -> none  [the longest x3 7.52 us: row_scale(): return lax.rsqrt(jnp.mean(wide * wide, axis=-1, keepdims=True) + 1e-06)]
    unnamed x43 -> x2, local copies, waits for them, and re-layouts: 7.79 us -> 3.2 us
  transfers between devices with their start and end apart: 10 -> 0, of which waited for: 8 -> 0; matrix products, arithmetic and copies ran while one was open for 9% -> 0% of each run, Pallas kernels for 0% -> 0%
where the time goes in v2:
time: 144 us
  Pallas kernels  140 us (97%)
  local copies, waits for them, and re-layouts  3.2 us (2%)
    pallas_call x1, Pallas kernels, shards(): pl.pallas_call(functools.partial(layer_kernel, n_seq, n_head), out_shape=...  140 us
    unnamed x2, local copies, waits for them, and re-layouts  3.2 us

profile of v2, /device:TPU:1, one launch (start us, length us, event | category | flops | bytes accessed | tf_op | source)
XLA Modules:
  0.0 143.7 jit_solution(9002938568249355149)
XLA Ops:
  0.0 1.5 %copy.13.ids_col = s32[512,1]{1,0:T(8,128)} copy(s32[512,1]{0,1:T(1,128)} %param.23) | data formatting | bytes 4096 | tf_op args[11]
  1.5 140.5 %shard_map.118 = bf16[512,256]{1,0:T(8,128)(2,1)} custom-call(bf16[512,2048]{1,0:T(8,128)(2,1)} %tok.1, bf16[2048,256]{1,0:T(8,128)(2,1)} %wq.1, bf16[2048,256]{1,0:T(8,128)(2,1)} %wk.1, bf16[2048,256]{1,0:T(8,128)(2,1)} %wv.1, bf16[256,2048]{1,0:T(8,128)(2,1)} %wo.1, bf16[2048,128]{1,0:T(8,128)(2,1)} %sg.1, bf16[2048,128]{1,0:T(8,128)(2,1)} %su.1, ...), custom_call_target="tpu_custom_call" | custom-call | tf_op jit(solution)/shard_map/pallas_call | solution.py:454
  142.0 1.7 %copy.15 = bf16[512,256]{1,0:T(8,128)(2,1)} copy(bf16[512,256]{1,0:T(8,128)(2,1)} %shard_map.118) | data formatting | bytes 524288

commit v3 on v2

v3 whole, which is shorter than its diff:
```python
import functools

import jax
import jax.numpy as jnp
from jax import lax
from jax.experimental import pallas as pl
from jax.experimental.pallas import tpu as pltpu
from jax.sharding import PartitionSpec as P

HD = 128
CAP = 16
NY = 4
F32 = jnp.float32
BF16 = jnp.bfloat16

STATE, CARRY, DISPATCH, RETURN = 0, 1, 2, 4
EXCHANGES = 6
HEADS, MIDDLE, ROUTED, SHARED_HIDDEN, ROUTED_HIDDEN = 0, 1, 2, 4, 5
GATHERS = 7


def dot(a, b, contract=((1,), (0,))):
    return lax.dot_general(a, b, (contract, ((), ())), preferred_element_type=F32)


def two_part(values):
    high = values.astype(BF16)
    return high, (values - high.astype(F32)).astype(BF16)


def rms(total, count):
    return lax.rsqrt(total * (1.0 / count) + 1e-06)


def silu(v):
    return v / (1.0 + jnp.exp(-v))


def layer_kernel(
    n_seq, n_head,
    tok, wq, wk, wv, wo, sg, su, sd, eg, eu, ed, ids_row,
    out,
    x, own, wqkv, wo_v, sd_v, ed_v, sgu, egu, qkv, st, got, pre, car, att,
    hn, mid, rin, outb, hs, hr, rout, back, res, chosen, chosen_t, acc, sq,
    load_sem, w_send, w_recv, s_send, s_recv, g_send, g_recv,
):
    rows, width = x.shape
    cols = width // n_head
    owned = eg.shape[0]
    hidden = eg.shape[2]
    span = 2 * HD
    per = n_seq // 2
    s = lax.axis_index("seq")
    h = lax.axis_index("head")
    core = h % 2
    chip = h // 2
    chips = n_head // 2
    deep = n_seq // NY
    lay = s // deep
    partner = 2 * chip + 1 - core
    right = 2 * ((chip + 1) % chips) + core
    left = 2 * ((chip + chips - 1) % chips) + core
    far = 2 * ((chip + 2) % chips) + core

    def twin(b):
        return 2 * (b // 2) + 1 - b % 2

    def col_slice(index, size):
        return pl.ds(pl.multiple_of(index * size, 128), size)

    def load(i, src, dst):
        return pltpu.make_async_copy(src, dst, load_sem.at[i])

    loads = [
        load(0, tok, x),
        load(1, wq, wqkv.at[:, pl.ds(0, span)]),
        load(2, wk, wqkv.at[:, pl.ds(span, span)]),
        load(3, wv, wqkv.at[:, pl.ds(2 * span, span)]),
        load(4, tok.at[:, col_slice(h, cols)], own),
        load(5, wo.at[:, col_slice(h, cols)], wo_v.at[h]),
        load(6, sd.at[:, col_slice(h, cols)], sd_v.at[h]),
        load(7, ed.at[:, :, col_slice(h, cols)], ed_v.at[h]),
        load(8, sg, sgu.at[:, pl.ds(0, hidden)]),
        load(9, su, sgu.at[:, pl.ds(hidden, hidden)]),
        load(10, eg, egu.at[:, :, pl.ds(0, hidden)]),
        load(11, eu, egu.at[:, :, pl.ds(hidden, hidden)]),
    ]

    def seq_peer(t):
        return (s + t) % n_seq

    def head_peer(t):
        return (h + t) % n_head

    barrier = pltpu.get_barrier_semaphore()

    def greet_seq(t, carry):
        pl.semaphore_signal(barrier, inc=1, device_id={"seq": seq_peer(t)})
        return carry

    def greet_head(t, carry):
        pl.semaphore_signal(barrier, inc=1, device_id={"head": head_peer(t)})
        return carry

    for copy in loads[:4]:
        copy.start()
    lax.fori_loop(1, n_head, greet_head, 0)
    lax.fori_loop(1, n_seq, greet_seq, 0)
    for copy in loads[4:]:
        copy.start()

    def part_of(i):
        n = (wo_v, sd_v)[i].shape[1] // NY
        return pl.ds(pl.multiple_of(lay * n, n), n)

    def weight_copy(i, peer):
        at = col_slice(peer, cols)
        if i == 2:
            src, dst = ed.at[:, :, at], ed_v.at[h]
        else:
            src, dst = (wo, sd)[i].at[part_of(i), at], (wo_v, sd_v)[i].at[h, part_of(i)]
        return pltpu.make_async_remote_copy(
            src, dst, w_send.at[i], w_recv.at[i], device_id={"head": peer}
        )

    def weight_bytes(i):
        some = pl.ds(0, n_head - 1)
        if i == 2:
            ref = ed_v.at[some]
        elif i < 2:
            ref = (wo_v, sd_v)[i].at[some, pl.ds(0, (wo_v, sd_v)[i].shape[1] // NY)]
        else:
            whole = (wo_v, sd_v)[i - 3]
            ref = whole.at[some, pl.ds(0, whole.shape[1] // NY * (NY - 1))]
        return pltpu.make_async_remote_copy(
            ref, ref, w_send.at[i], w_recv.at[i], device_id={"head": partner}
        )

    def weight_share(i):
        whole = (wo_v, sd_v)[i]

        def one(t, carry):
            ref = whole.at[head_peer(t), part_of(i)]
            for k in (2, 1, 3):
                pltpu.make_async_remote_copy(
                    ref, ref, w_send.at[3 + i], w_recv.at[3 + i],
                    device_id={"seq": ((lay + k) % NY) * deep + s % deep},
                ).start()
            return carry

        lax.fori_loop(1, n_head, one, 0)

    def seq_refs(e):
        if e == STATE:
            return st, got
        if e == CARRY:
            return pre, car
        if e >= RETURN:
            return rout.at[e - RETURN], back.at[e - RETURN]
        return outb.at[e - DISPATCH], rin.at[h, e - DISPATCH]

    def seq_start(e):
        src, dst = seq_refs(e)

        def one(t, carry):
            peer = seq_peer(t)
            pltpu.make_async_remote_copy(
                src.at[peer], dst.at[s], s_send.at[e], s_recv.at[e], device_id={"seq": peer}
            ).start()
            return carry

        lax.fori_loop(1, n_seq, one, 0)

    def seq_bytes(e):
        src, dst = seq_refs(e)
        some = pl.ds(0, n_seq - 1)
        return pltpu.make_async_remote_copy(
            src.at[some], dst.at[some], s_send.at[e], s_recv.at[e],
            device_id={"seq": seq_peer(1)},
        )

    def view(g, b):
        if g == HEADS:
            return hn.at[b]
        if g == MIDDLE:
            return mid.at[b]
        if g == SHARED_HIDDEN:
            return hs.at[b]
        if g >= ROUTED_HIDDEN:
            return hr.at[b, g - ROUTED_HIDDEN]
        return rin.at[b, g - ROUTED]

    def half(g, b, k):
        whole = view(g, b)
        n = whole.shape[0] // 2
        return whole.at[pl.ds(k * n, n)]

    def leg(g, ref, i, target):
        return pltpu.make_async_remote_copy(
            ref, ref, g_send.at[g], g_recv.at[g, i], device_id={"head": target}
        )

    FROM_LEFT, FROM_RIGHT, FROM_TWIN, FAR, TWIN_LEFT, TWIN_RIGHT, TWIN_FAR = range(7)

    def arrived(g, i):
        b = (left, right, partner, far, twin(left), twin(right), twin(far))[i]
        leg(g, view(g, b), i, partner).wait_recv()
        return b

    def gather_start(g):
        leg(g, view(g, h), FROM_LEFT, right).start()
        leg(g, view(g, h), FROM_RIGHT, left).start()
        leg(g, view(g, h), FROM_TWIN, partner).start()

    def gather_pass(g):
        arrived(g, FROM_LEFT)
        leg(g, half(g, left, 0), FAR, right).start()
        leg(g, view(g, left), TWIN_LEFT, partner).start()
        arrived(g, FROM_RIGHT)
        leg(g, half(g, right, 1), FAR, left).start()
        leg(g, view(g, right), TWIN_RIGHT, partner).start()

    def gather_far(g):
        arrived(g, FAR)
        leg(g, view(g, far), TWIN_FAR, partner).start()

    def gather_sent(g):
        some = pl.ds(0, n_head - 1)
        ref = view(g, some)
        leg(g, ref, 0, partner).wait_send()

    for i in (0, 1, 2, 3):
        loads[i].wait()
    block = min(256, rows)

    def square_sum(ref, at, count):
        total = None
        for j in range(count // 128):
            wide = ref[at, j * 128 : (j + 1) * 128].astype(F32)
            total = wide * wide if total is None else total + wide * wide
        return total

    def project(i, carry):
        at = pl.ds(pl.multiple_of(i * block, block), block)
        scale = rms(jnp.sum(square_sum(x, at, width), axis=-1, keepdims=True), width)
        qkv[at, :] = (dot(x[at, :], wqkv[...]) * scale).astype(BF16)
        return carry

    lax.fori_loop(0, rows // block, project, 0)

    for a in range(2):
        k = qkv[:, span + a * HD : span + (a + 1) * HD]
        v = qkv[:, 2 * span + a * HD : 2 * span + (a + 1) * HD]
        st[a * per : (a + 1) * per] = dot(k, v, ((0,), (0,))).reshape(per, -1, HD)

    for a in range(2):
        for i in range(rows // block):
            top, end = i * block, (i + 1) * block
            q = qkv[top:end, a * HD : (a + 1) * HD]
            k = qkv[:end, span + a * HD : span + (a + 1) * HD]
            v = qkv[:end, 2 * span + a * HD : 2 * span + (a + 1) * HD]
            scores = dot(q, k, ((1,), (1,)))
            row = lax.broadcasted_iota(jnp.int32, scores.shape, 0) + top
            col = lax.broadcasted_iota(jnp.int32, scores.shape, 1)
            high, low = two_part(jnp.where(row >= col, scores, 0.0))
            att[top:end, a * HD : (a + 1) * HD] = dot(high, v) + dot(low, v)

    ids_r = ids_row[...]
    ids_c = jnp.transpose(jnp.broadcast_to(ids_r.astype(F32), (128, rows)))[:, :1].astype(jnp.int32)
    row = lax.broadcasted_iota(jnp.int32, (rows, rows), 0)
    col = lax.broadcasted_iota(jnp.int32, (rows, rows), 1)
    same = ids_c == ids_r
    rank_r = jnp.sum(jnp.where(same & (row <= col), 1.0, 0.0), axis=0, keepdims=True)
    rank_c = jnp.sum(jnp.where(same & (col <= row), 1.0, 0.0), axis=1, keepdims=True)
    taken = n_seq * CAP
    slots = owned * taken

    def base(ids, rank):
        place = (ids & 1) * taken + (ids >> 1) * CAP
        return place.astype(F32) + (rank - 1.0)

    place = lax.broadcasted_iota(jnp.int32, (slots, 1), 0).astype(F32)
    chosen[...] = jnp.where(place == base(ids_r, rank_r), 1.0, 0.0).astype(BF16)
    place = lax.broadcasted_iota(jnp.int32, (1, slots), 1).astype(F32)
    chosen_t[...] = jnp.where(place == base(ids_c, rank_c), 1.0, 0.0).astype(BF16)

    pl.semaphore_wait(barrier, n_head - 1 + n_seq - 1)
    for i in range(3):

        def one(t, carry):
            weight_copy(i, head_peer(t)).start()
            return carry

        lax.fori_loop(1, n_head, one, 0)
    seq_start(STATE)
    got[s] = st[s]
    seq_bytes(STATE).wait_recv()

    def running(j, total):
        pre[j] = total
        return total + got[j]

    lax.fori_loop(0, n_seq, running, jnp.zeros(pre.shape[1:], F32))
    seq_start(CARRY)
    car[s] = pre[s]
    weight_bytes(0).wait_recv()
    weight_share(0)

    seq_bytes(CARRY).wait_recv()
    for a in range(2):
        high, low = two_part(car[a * per : (a + 1) * per].reshape(HD, HD))
        q = qkv[:, a * HD : (a + 1) * HD]
        whole = att[:, a * HD : (a + 1) * HD] + dot(q, high) + dot(q, low)
        scale = rms(jnp.sum(whole * whole, axis=-1, keepdims=True), HD)
        hn[h, :, a * HD : (a + 1) * HD] = (whole * scale).astype(BF16)
    gather_start(HEADS)

    loads[4].wait()
    res[...] = own[...].astype(F32)
    loads[5].wait()
    weight_bytes(3).wait_recv()

    def use_heads(b):
        res[...] += dot(hn[b], wo_v[b])

    use_heads(h)
    use_heads(arrived(HEADS, FROM_TWIN))
    gather_pass(HEADS)
    use_heads(left)
    use_heads(right)
    gather_far(HEADS)
    use_heads(far)
    for i in (TWIN_LEFT, TWIN_RIGHT, TWIN_FAR):
        use_heads(arrived(HEADS, i))
    mid[h] = res[...].astype(BF16)
    gather_start(MIDDLE)
    for e in range(owned):
        picked = dot(chosen[e * taken : (e + 1) * taken, :], mid[h])
        outb[e] = picked.astype(BF16).reshape(outb.shape[1:])
        seq_start(DISPATCH + e)
        rin[h, e, s] = outb[e, s]
    weight_bytes(1).wait_recv()
    weight_share(1)

    loads[8].wait()
    loads[9].wait()
    acc[...] = jnp.zeros_like(acc)
    sq[...] = jnp.zeros_like(sq)

    def columns_of(b):
        return pl.ds(pl.multiple_of(b * cols, cols), cols)

    def add_squares(slot, part):
        wide = part.astype(F32)
        wide = wide * wide
        total = wide[:, :128]
        for j in range(1, cols // 128):
            total += wide[:, j * 128 : (j + 1) * 128]
        sq[slot, pl.ds(0, part.shape[0]), :] += total

    def use_middle(b):
        part = mid[b]
        acc[0, pl.ds(0, rows), :] += dot(part, sgu[columns_of(b), :])
        add_squares(0, part)

    def use_routed(e, b):
        part = rin[b, e].reshape(taken, cols)
        acc[1 + e, pl.ds(0, taken), :] += dot(part, egu[e, columns_of(b), :])
        add_squares(1 + e, part)

    def activate(slot, count):
        at = pl.ds(0, count)
        scale = rms(jnp.sum(sq[slot, at, :], axis=-1, keepdims=True), width)
        gate = acc[slot, at, pl.ds(0, hidden)] * scale
        up = acc[slot, at, pl.ds(hidden, hidden)] * scale
        return (silu(gate) * up).astype(BF16)

    use_middle(h)
    use_middle(arrived(MIDDLE, FROM_TWIN))
    gather_pass(MIDDLE)
    use_middle(left)
    use_middle(right)
    seq_bytes(DISPATCH).wait_recv()
    gather_start(ROUTED)
    gather_far(MIDDLE)
    use_middle(far)
    for i in (TWIN_LEFT, TWIN_RIGHT, TWIN_FAR):
        use_middle(arrived(MIDDLE, i))
    hs[h] = activate(0, rows)
    gather_start(SHARED_HIDDEN)

    loads[10].wait()
    loads[11].wait()
    use_routed(0, h)
    gather_pass(ROUTED)
    seq_bytes(DISPATCH + 1).wait_recv()
    gather_start(ROUTED + 1)
    use_routed(0, arrived(ROUTED, FROM_TWIN))
    use_routed(0, left)
    use_routed(0, right)
    gather_pass(SHARED_HIDDEN)
    gather_far(ROUTED)
    use_routed(0, far)
    for i in (TWIN_LEFT, TWIN_RIGHT, TWIN_FAR):
        use_routed(0, arrived(ROUTED, i))
    hr[h, 0] = activate(1, taken)
    gather_pass(ROUTED + 1)
    gather_start(ROUTED_HIDDEN)
    use_routed(1, h)
    use_routed(1, arrived(ROUTED + 1, FROM_TWIN))
    use_routed(1, left)
    use_routed(1, right)
    gather_far(SHARED_HIDDEN)
    gather_far(ROUTED + 1)
    use_routed(1, far)
    for i in (TWIN_LEFT, TWIN_RIGHT, TWIN_FAR):
        use_routed(1, arrived(ROUTED + 1, i))
    hr[h, 1] = activate(2, taken)
    gather_start(ROUTED_HIDDEN + 1)

    loads[6].wait()
    loads[7].wait()
    weight_bytes(2).wait_recv()

    def use_shared(b):
        res[...] += dot(hs[b], sd_v[b])

    def use_hidden(e, b):
        acc[1 + e, pl.ds(0, taken), pl.ds(0, cols)] += dot(hr[b, e], ed_v[b, e])

    for e in range(owned):
        acc[1 + e] = jnp.zeros(acc.shape[1:], F32)
    gather_pass(ROUTED_HIDDEN)
    use_hidden(0, h)
    use_hidden(0, arrived(ROUTED_HIDDEN, FROM_TWIN))
    use_hidden(0, left)
    use_hidden(0, right)
    gather_far(ROUTED_HIDDEN)
    gather_pass(ROUTED_HIDDEN + 1)
    use_hidden(0, far)
    for i in (TWIN_LEFT, TWIN_RIGHT, TWIN_FAR):
        use_hidden(0, arrived(ROUTED_HIDDEN, i))

    def give_back(e):
        result = acc[1 + e, pl.ds(0, taken), pl.ds(0, cols)]
        rout[e] = result.astype(BF16).reshape(rout.shape[1:])
        seq_start(RETURN + e)
        back[e, s] = rout[e, s]

    give_back(0)
    use_hidden(1, h)
    use_hidden(1, arrived(ROUTED_HIDDEN + 1, FROM_TWIN))
    use_hidden(1, left)
    use_hidden(1, right)
    gather_far(ROUTED_HIDDEN + 1)
    use_hidden(1, far)
    for i in (TWIN_LEFT, TWIN_RIGHT, TWIN_FAR):
        use_hidden(1, arrived(ROUTED_HIDDEN + 1, i))
    give_back(1)

    weight_bytes(4).wait_recv()
    for b in (h, left, right, far):
        use_shared(b)
    for i in (FROM_TWIN, TWIN_LEFT, TWIN_RIGHT, TWIN_FAR):
        use_shared(arrived(SHARED_HIDDEN, i))
    seq_bytes(RETURN).wait_recv()
    res[...] += dot(chosen_t[:, :taken], back[0].reshape(taken, cols))
    seq_bytes(RETURN + 1).wait_recv()
    routed = dot(chosen_t[:, taken:], back[1].reshape(taken, cols))
    out[...] = (res[...] + routed).astype(BF16)

    for i in range(5):
        weight_bytes(i).wait_send()
    for e in range(EXCHANGES):
        seq_bytes(e).wait_send()
    for g in range(GATHERS):
        gather_sent(g)


def shards(
    tokens,
    w_query,
    w_key,
    w_value,
    w_out,
    shared_gate,
    shared_up,
    shared_down,
    expert_gate,
    expert_up,
    expert_down,
    expert_ids,
):
    n_seq, n_head = lax.axis_size("seq"), lax.axis_size("head")
    rows, width = tokens.shape
    cols = width // n_head
    owned, _, hidden = expert_gate.shape
    heads = w_query.shape[1]
    taken = n_seq * CAP
    slots = owned * taken
    chunk = heads // n_seq
    most = max(rows, taken)
    any_spec = pl.BlockSpec(memory_space=pl.ANY)
    vmem_spec = pl.BlockSpec(memory_space=pltpu.VMEM)
    V = pltpu.VMEM
    dma = pltpu.SemaphoreType.DMA
    return pl.pallas_call(
        functools.partial(layer_kernel, n_seq, n_head),
        out_shape=jax.ShapeDtypeStruct((rows, cols), BF16),
        in_specs=[any_spec] * 11 + [vmem_spec],
        out_specs=vmem_spec,
        scratch_shapes=[
            V((rows, width), BF16),
            V((rows, cols), BF16),
            V((width, 3 * heads), BF16),
            V((n_head, heads, cols), BF16),
            V((n_head, hidden, cols), BF16),
            V((n_head, owned, hidden, cols), BF16),
            V((width, 2 * hidden), BF16),
            V((owned, width, 2 * hidden), BF16),
            V((rows, 3 * heads), BF16),
            V((n_seq, chunk, HD), F32),
            V((n_seq, chunk, HD), F32),
            V((n_seq, chunk, HD), F32),
            V((n_seq, chunk, HD), F32),
            V((rows, heads), F32),
            V((n_head, rows, heads), BF16),
            V((n_head, rows, cols), BF16),
            V((n_head, owned, n_seq, CAP, cols), BF16),
            V((owned, n_seq, CAP, cols), BF16),
            V((n_head, rows, hidden), BF16),
            V((n_head, owned, taken, hidden), BF16),
            V((owned, n_seq, CAP, cols), BF16),
            V((owned, n_seq, CAP, cols), BF16),
            V((rows, cols), F32),
            V((slots, rows), BF16),
            V((rows, slots), BF16),
            V((1 + owned, most, 2 * hidden), F32),
            V((1 + owned, most, HD), F32),
            dma((12,)),
            dma((5,)),
            dma((5,)),
            dma((EXCHANGES,)),
            dma((EXCHANGES,)),
            dma((GATHERS,)),
            dma((GATHERS, 7)),
        ],
        compiler_params=pltpu.CompilerParams(
            collective_id=0, has_side_effects=True, vmem_limit_bytes=60 * 1024 * 1024
        ),
    )(
        tokens, w_query, w_key, w_value, w_out, shared_gate, shared_up, shared_down,
        expert_gate, expert_up, expert_down, expert_ids.reshape(1, rows),
    )


def solution(mesh):
    return jax.shard_map(
        shards,
        mesh=mesh,
        in_specs=(
            P("seq", None),
            P(None, "head"),
            P(None, "head"),
            P(None, "head"),
            P("head", None),
            P(None, "head"),
            P(None, "head"),
            P("head", None),
            P("seq", None, "head"),
            P("seq", None, "head"),
            P("seq", "head", None),
            P("seq", None),
        ),
        out_specs=P("seq", "head"),
        check_vma=False,
    )
```

time: 144 us -> 107 us (0.74)
  Pallas kernels: 140 us -> 105 us
  local copies, waits for them, and re-layouts: 3.2 us -> 1.67 us
    pallas_call x1, Pallas kernels: 140 us -> 105 us  [shards(): pl.pallas_call(functools.partial(layer_kernel, n_seq, n_head), out_shape=...]
    unnamed x2 -> x1, local copies, waits for them, and re-layouts: 3.2 us -> 1.67 us
where the time goes in v3:
time: 107 us
  Pallas kernels  105 us (98%)
  local copies, waits for them, and re-layouts  1.67 us (2%)
    pallas_call x1, Pallas kernels, shards(): pl.pallas_call(functools.partial(layer_kernel, n_seq, n_head), out_shape=...  105 us

profile of v3, /device:TPU:1, one launch (start us, length us, event | category | flops | bytes accessed | tf_op | source)
XLA Modules:
  0.0 106.7 jit_solution(3389696283717561161)
XLA Ops:
  0.0 105.0 %shard_map.118 = bf16[512,256]{1,0:T(8,128)(2,1)} custom-call(bf16[512,2048]{1,0:T(8,128)(2,1)} %tok.1, bf16[2048,256]{1,0:T(8,128)(2,1)} %wq.1, bf16[2048,256]{1,0:T(8,128)(2,1)} %wk.1, bf16[2048,256]{1,0:T(8,128)(2,1)} %wv.1, bf16[256,2048]{1,0:T(8,128)(2,1)} %wo.1, bf16[2048,128]{1,0:T(8,128)(2,1)} %sg.1, bf16[2048,128]{1,0:T(8,128)(2,1)} %su.1, ...), custom_call_target="tpu_custom_call" | custom-call | tf_op jit(solution)/shard_map/pallas_call | solution.py:507
  105.1 1.7 %copy.14 = bf16[512,256]{1,0:T(8,128)(2,1)} copy(bf16[512,256]{1,0:T(8,128)(2,1)} %shard_map.118) | data formatting | bytes 524288

commit v4 on v3

--- a/solution.py
+++ b/solution.py
@@ -10,13 +10,15 @@
 HD = 128
 CAP = 16
 NY = 4
+AHEAD = 4
+LOTS = ((0, 0), (0, 1), (1, 0), (1, 1))
 F32 = jnp.float32
 BF16 = jnp.bfloat16
 
-STATE, CARRY, DISPATCH, RETURN = 0, 1, 2, 4
-EXCHANGES = 6
-HEADS, MIDDLE, ROUTED, SHARED_HIDDEN, ROUTED_HIDDEN = 0, 1, 2, 4, 5
-GATHERS = 7
+STATE, CARRY, DISPATCH, RETURN = 0, 1, 2, 6
+EXCHANGES = 8
+HEADS, MIDDLE, SHARED_HIDDEN, ROUTED, ROUTED_HIDDEN = 0, 2, 4, 5, 9
+GATHERS = 13
 
 
 def dot(a, b, contract=((1,), (0,))):
@@ -115,8 +117,10 @@
 
     def weight_copy(i, peer):
         at = col_slice(peer, cols)
-        if i == 2:
-            src, dst = ed.at[:, :, at], ed_v.at[h]
+        if i >= 5:
+            e, part = LOTS[i - 5]
+            part = pl.ds(part * (hidden // 2), hidden // 2)
+            src, dst = ed.at[e, part, at], ed_v.at[h, e, part]
         else:
             src, dst = (wo, sd)[i].at[part_of(i), at], (wo_v, sd_v)[i].at[h, part_of(i)]
         return pltpu.make_async_remote_copy(
@@ -125,8 +129,8 @@
 
     def weight_bytes(i):
         some = pl.ds(0, n_head - 1)
-        if i == 2:
-            ref = ed_v.at[some]
+        if i >= 5:
+            ref = ed_v.at[some, 0, pl.ds(0, hidden // 2)]
         elif i < 2:
             ref = (wo_v, sd_v)[i].at[some, pl.ds(0, (wo_v, sd_v)[i].shape[1] // NY)]
         else:
@@ -136,7 +140,7 @@
             ref, ref, w_send.at[i], w_recv.at[i], device_id={"head": partner}
         )
 
-    def weight_share(i):
+    def weight_share(i, first=1, end=None):
         whole = (wo_v, sd_v)[i]
 
         def one(t, carry):
@@ -148,47 +152,56 @@
                 ).start()
             return carry
 
-        lax.fori_loop(1, n_head, one, 0)
-
-    def seq_refs(e):
+        lax.fori_loop(first, end or n_head, one, 0)
+
+    def seq_refs(e, peer):
         if e == STATE:
-            return st, got
+            return st.at[peer], got.at[s]
         if e == CARRY:
-            return pre, car
+            return pre.at[peer], car.at[s]
         if e >= RETURN:
-            return rout.at[e - RETURN], back.at[e - RETURN]
-        return outb.at[e - DISPATCH], rin.at[h, e - DISPATCH]
-
-    def seq_start(e):
-        src, dst = seq_refs(e)
-
+            return rout.at[e - RETURN, peer % 2, peer // 2], back.at[e - RETURN, s]
+        e = (e - DISPATCH) // 2
+        return outb.at[e, peer], rin.at[h, e, s % 2, s // 2]
+
+    def seq_send(e, first, last, stride):
         def one(t, carry):
-            peer = seq_peer(t)
+            peer = seq_peer(t * stride + first)
+            src, dst = seq_refs(e, peer)
             pltpu.make_async_remote_copy(
-                src.at[peer], dst.at[s], s_send.at[e], s_recv.at[e], device_id={"seq": peer}
+                src, dst, s_send.at[e], s_recv.at[e], device_id={"seq": peer}
             ).start()
             return carry
 
-        lax.fori_loop(1, n_seq, one, 0)
+        lax.fori_loop(0, last, one, 0)
+
+    def seq_start(e):
+        seq_send(e, 1, n_seq - 1, 1)
 
     def seq_bytes(e):
-        src, dst = seq_refs(e)
-        some = pl.ds(0, n_seq - 1)
+        ref = st if e == STATE else pre if e == CARRY else back.at[0]
+        count = n_seq - 1
+        if DISPATCH <= e < RETURN:
+            count = n_seq // 2 - 1 + e % 2
+        ref = ref.at[pl.ds(0, count)]
         return pltpu.make_async_remote_copy(
-            src.at[some], dst.at[some], s_send.at[e], s_recv.at[e],
-            device_id={"seq": seq_peer(1)},
+            ref, ref, s_send.at[e], s_recv.at[e], device_id={"seq": seq_peer(1)}
         )
 
+    parity = s % 2
+    middle = rows // 2
+
+    def lot(c):
+        return c // 2, (parity + c) % 2
+
     def view(g, b):
-        if g == HEADS:
-            return hn.at[b]
-        if g == MIDDLE:
-            return mid.at[b]
+        if g < SHARED_HIDDEN:
+            ref = hn if g < MIDDLE else mid
+            return ref.at[b, pl.ds(g % 2 * middle, middle)]
         if g == SHARED_HIDDEN:
             return hs.at[b]
-        if g >= ROUTED_HIDDEN:
-            return hr.at[b, g - ROUTED_HIDDEN]
-        return rin.at[b, g - ROUTED]
+        e, side = lot((g - ROUTED) % 4)
+        return (rin if g < ROUTED_HIDDEN else hr).at[b, e, side]
 
     def half(g, b, k):
         whole = view(g, b)
@@ -285,15 +298,19 @@
     chosen_t[...] = jnp.where(place == base(ids_c, rank_c), 1.0, 0.0).astype(BF16)
 
     pl.semaphore_wait(barrier, n_head - 1 + n_seq - 1)
-    for i in range(3):
-
+    seq_start(STATE)
+    got[s] = st[s]
+    def weight_start(i):
         def one(t, carry):
             weight_copy(i, head_peer(t)).start()
             return carry
 
         lax.fori_loop(1, n_head, one, 0)
-    seq_start(STATE)
-    got[s] = st[s]
+
+    weight_start(0)
+    weight_start(1)
+    for i in range(5, 5 + AHEAD):
+        weight_start(i)
     seq_bytes(STATE).wait_recv()
 
     def running(j, total):
@@ -314,31 +331,45 @@
         scale = rms(jnp.sum(whole * whole, axis=-1, keepdims=True), HD)
         hn[h, :, a * HD : (a + 1) * HD] = (whole * scale).astype(BF16)
     gather_start(HEADS)
+    gather_start(HEADS + 1)
 
     loads[4].wait()
     res[...] = own[...].astype(F32)
+    for k in range(2):
+        gather_pass(HEADS + k)
     loads[5].wait()
     weight_bytes(3).wait_recv()
 
-    def use_heads(b):
-        res[...] += dot(hn[b], wo_v[b])
-
-    use_heads(h)
-    use_heads(arrived(HEADS, FROM_TWIN))
-    gather_pass(HEADS)
-    use_heads(left)
-    use_heads(right)
-    gather_far(HEADS)
-    use_heads(far)
-    for i in (TWIN_LEFT, TWIN_RIGHT, TWIN_FAR):
-        use_heads(arrived(HEADS, i))
-    mid[h] = res[...].astype(BF16)
-    gather_start(MIDDLE)
+    def use_heads(k, b):
+        at = pl.ds(k * middle, middle)
+        res[at, :] += dot(hn[b, at, :], wo_v[b])
+
+    for k in range(2):
+        use_heads(k, h)
+        use_heads(k, arrived(HEADS + k, FROM_TWIN))
+        use_heads(k, left)
+        use_heads(k, right)
+    for k in range(2):
+        gather_far(HEADS + k)
+        use_heads(k, far)
+        for i in (TWIN_LEFT, TWIN_RIGHT, TWIN_FAR):
+            use_heads(k, arrived(HEADS + k, i))
+        at = pl.ds(k * middle, middle)
+        mid[h, at, :] = res[at, :].astype(BF16)
+        gather_start(MIDDLE + k)
+        if k == 0:
+            for e in range(owned):
+                own_lot = pl.ds(e * taken, taken)
+                acc[1 + e, pl.ds(0, taken), pl.ds(0, cols)] = dot(chosen[own_lot, at], mid[h, at, :])
     for e in range(owned):
-        picked = dot(chosen[e * taken : (e + 1) * taken, :], mid[h])
+        at = pl.ds(middle, middle)
+        picked = acc[1 + e, pl.ds(0, taken), pl.ds(0, cols)] + dot(
+            chosen[pl.ds(e * taken, taken), at], mid[h, at, :]
+        )
         outb[e] = picked.astype(BF16).reshape(outb.shape[1:])
-        seq_start(DISPATCH + e)
-        rin[h, e, s] = outb[e, s]
+        seq_send(DISPATCH + 2 * e, 2, n_seq // 2 - 1, 2)
+        seq_send(DISPATCH + 2 * e + 1, 1, n_seq // 2, 2)
+        rin[h, e, s % 2, s // 2] = outb[e, s]
     weight_bytes(1).wait_recv()
     weight_share(1)
 
@@ -350,115 +381,148 @@
     def columns_of(b):
         return pl.ds(pl.multiple_of(b * cols, cols), cols)
 
-    def add_squares(slot, part):
+    def add_squares(slot, top, part):
         wide = part.astype(F32)
         wide = wide * wide
         total = wide[:, :128]
         for j in range(1, cols // 128):
             total += wide[:, j * 128 : (j + 1) * 128]
-        sq[slot, pl.ds(0, part.shape[0]), :] += total
-
-    def use_middle(b):
-        part = mid[b]
-        acc[0, pl.ds(0, rows), :] += dot(part, sgu[columns_of(b), :])
-        add_squares(0, part)
-
-    def use_routed(e, b):
-        part = rin[b, e].reshape(taken, cols)
-        acc[1 + e, pl.ds(0, taken), :] += dot(part, egu[e, columns_of(b), :])
-        add_squares(1 + e, part)
-
-    def activate(slot, count):
-        at = pl.ds(0, count)
+        sq[slot, pl.ds(top, part.shape[0]), :] += total
+
+    def use_middle(k, b):
+        at = pl.ds(k * middle, middle)
+        part = mid[b, at, :]
+        acc[0, at, :] += dot(part, sgu[columns_of(b), :])
+        add_squares(0, k * middle, part)
+
+    lot_rows = taken // 2
+
+    def use_routed(c, b):
+        e, side = lot(c)
+        part = rin[b, e, side].reshape(lot_rows, cols)
+        acc[1 + e, pl.ds(c % 2 * lot_rows, lot_rows), :] += dot(part, egu[e, columns_of(b), :])
+        add_squares(1 + e, c % 2 * lot_rows, part)
+
+    def activate(slot, top, count):
+        at = pl.ds(top, count)
         scale = rms(jnp.sum(sq[slot, at, :], axis=-1, keepdims=True), width)
         gate = acc[slot, at, pl.ds(0, hidden)] * scale
         up = acc[slot, at, pl.ds(hidden, hidden)] * scale
         return (silu(gate) * up).astype(BF16)
 
-    use_middle(h)
-    use_middle(arrived(MIDDLE, FROM_TWIN))
+    near = (left, right)
+    last = (TWIN_LEFT, TWIN_RIGHT, TWIN_FAR)
+
+    def begin(g, use):
+        use(h)
+        use(arrived(g, FROM_TWIN))
+        for b in near:
+            use(b)
+
+    def end(g, use):
+        use(far)
+        for i in last:
+            use(arrived(g, i))
+
+    def routed(c):
+        return functools.partial(use_routed, c)
+
+    def hidden_of(c):
+        e, side = lot(c)
+        hr[h, e, side] = activate(1 + e, c % 2 * lot_rows, lot_rows)
+        gather_start(ROUTED_HIDDEN + c)
+
+    def shared(k):
+        return functools.partial(use_middle, k)
+
     gather_pass(MIDDLE)
-    use_middle(left)
-    use_middle(right)
+    begin(MIDDLE, shared(0))
+    gather_pass(MIDDLE + 1)
+    for i in range(5 + AHEAD, 9):
+        weight_start(i)
     seq_bytes(DISPATCH).wait_recv()
     gather_start(ROUTED)
     gather_far(MIDDLE)
-    use_middle(far)
-    for i in (TWIN_LEFT, TWIN_RIGHT, TWIN_FAR):
-        use_middle(arrived(MIDDLE, i))
-    hs[h] = activate(0, rows)
-    gather_start(SHARED_HIDDEN)
-
+    begin(MIDDLE + 1, shared(1))
+    seq_bytes(DISPATCH + 1).wait_recv()
+    gather_start(ROUTED + 1)
+    end(MIDDLE, shared(0))
+    gather_far(MIDDLE + 1)
+    end(MIDDLE + 1, shared(1))
+    hs[h] = activate(0, 0, rows)
+    gather_pass(ROUTED)
+    seq_bytes(DISPATCH + 2).wait_recv()
+    gather_start(ROUTED + 2)
     loads[10].wait()
     loads[11].wait()
-    use_routed(0, h)
-    gather_pass(ROUTED)
-    seq_bytes(DISPATCH + 1).wait_recv()
-    gather_start(ROUTED + 1)
-    use_routed(0, arrived(ROUTED, FROM_TWIN))
-    use_routed(0, left)
-    use_routed(0, right)
-    gather_pass(SHARED_HIDDEN)
+    begin(ROUTED, routed(0))
+    gather_pass(ROUTED + 1)
+    seq_bytes(DISPATCH + 3).wait_recv()
+    gather_start(ROUTED + 3)
     gather_far(ROUTED)
-    use_routed(0, far)
-    for i in (TWIN_LEFT, TWIN_RIGHT, TWIN_FAR):
-        use_routed(0, arrived(ROUTED, i))
-    hr[h, 0] = activate(1, taken)
-    gather_pass(ROUTED + 1)
-    gather_start(ROUTED_HIDDEN)
-    use_routed(1, h)
-    use_routed(1, arrived(ROUTED + 1, FROM_TWIN))
-    use_routed(1, left)
-    use_routed(1, right)
-    gather_far(SHARED_HIDDEN)
+    end(ROUTED, routed(0))
+    hidden_of(0)
+    begin(ROUTED + 1, routed(1))
+    gather_pass(ROUTED + 2)
     gather_far(ROUTED + 1)
-    use_routed(1, far)
-    for i in (TWIN_LEFT, TWIN_RIGHT, TWIN_FAR):
-        use_routed(1, arrived(ROUTED + 1, i))
-    hr[h, 1] = activate(2, taken)
-    gather_start(ROUTED_HIDDEN + 1)
+    end(ROUTED + 1, routed(1))
+    hidden_of(1)
+    gather_pass(ROUTED_HIDDEN)
+    begin(ROUTED + 2, routed(2))
+    gather_pass(ROUTED + 3)
+    gather_far(ROUTED + 2)
+    end(ROUTED + 2, routed(2))
+    hidden_of(2)
 
     loads[6].wait()
     loads[7].wait()
-    weight_bytes(2).wait_recv()
+    for i in range(5, 9):
+        weight_bytes(i).wait_recv()
 
     def use_shared(b):
         res[...] += dot(hs[b], sd_v[b])
 
-    def use_hidden(e, b):
-        acc[1 + e, pl.ds(0, taken), pl.ds(0, cols)] += dot(hr[b, e], ed_v[b, e])
-
-    for e in range(owned):
-        acc[1 + e] = jnp.zeros(acc.shape[1:], F32)
-    gather_pass(ROUTED_HIDDEN)
-    use_hidden(0, h)
-    use_hidden(0, arrived(ROUTED_HIDDEN, FROM_TWIN))
-    use_hidden(0, left)
-    use_hidden(0, right)
+    def give_back(c):
+        e, side = lot(c)
+        total = None
+        for b in (h, left, right, far, partner, twin(left), twin(right), twin(far)):
+            part = dot(hr[b, e, side], ed_v[b, e])
+            total = part if total is None else total + part
+        rout[e, side] = total.astype(BF16).reshape(rout.shape[2:])
+        if c % 2 == 0:
+            seq_send(RETURN + e, 2, n_seq // 2 - 1, 2)
+            back[e, s] = rout[e, side, s // 2]
+        else:
+            seq_send(RETURN + e, 1, n_seq // 2, 2)
+
+    def hidden_end(c):
+        for i in (FROM_TWIN,) + last:
+            arrived(ROUTED_HIDDEN + c, i)
+
     gather_far(ROUTED_HIDDEN)
     gather_pass(ROUTED_HIDDEN + 1)
-    use_hidden(0, far)
-    for i in (TWIN_LEFT, TWIN_RIGHT, TWIN_FAR):
-        use_hidden(0, arrived(ROUTED_HIDDEN, i))
-
-    def give_back(e):
-        result = acc[1 + e, pl.ds(0, taken), pl.ds(0, cols)]
-        rout[e] = result.astype(BF16).reshape(rout.shape[1:])
-        seq_start(RETURN + e)
-        back[e, s] = rout[e, s]
-
+    hidden_end(0)
     give_back(0)
-    use_hidden(1, h)
-    use_hidden(1, arrived(ROUTED_HIDDEN + 1, FROM_TWIN))
-    use_hidden(1, left)
-    use_hidden(1, right)
+    begin(ROUTED + 3, routed(3))
+    gather_far(ROUTED + 3)
+    end(ROUTED + 3, routed(3))
+    hidden_of(3)
     gather_far(ROUTED_HIDDEN + 1)
-    use_hidden(1, far)
-    for i in (TWIN_LEFT, TWIN_RIGHT, TWIN_FAR):
-        use_hidden(1, arrived(ROUTED_HIDDEN + 1, i))
+    gather_pass(ROUTED_HIDDEN + 2)
+    hidden_end(1)
     give_back(1)
+    gather_far(ROUTED_HIDDEN + 2)
+    gather_pass(ROUTED_HIDDEN + 3)
+    gather_start(SHARED_HIDDEN)
+    hidden_end(2)
+    give_back(2)
+    gather_far(ROUTED_HIDDEN + 3)
+    hidden_end(3)
+    give_back(3)
 
     weight_bytes(4).wait_recv()
+    gather_pass(SHARED_HIDDEN)
+    gather_far(SHARED_HIDDEN)
     for b in (h, left, right, far):
         use_shared(b)
     for i in (FROM_TWIN, TWIN_LEFT, TWIN_RIGHT, TWIN_FAR):
@@ -466,10 +530,10 @@
     seq_bytes(RETURN).wait_recv()
     res[...] += dot(chosen_t[:, :taken], back[0].reshape(taken, cols))
     seq_bytes(RETURN + 1).wait_recv()
-    routed = dot(chosen_t[:, taken:], back[1].reshape(taken, cols))
-    out[...] = (res[...] + routed).astype(BF16)
-
-    for i in range(5):
+    final = dot(chosen_t[:, taken:], back[1].reshape(taken, cols))
+    out[...] = (res[...] + final).astype(BF16)
+
+    for i in (0, 1, 3, 4, 5, 6, 7, 8):
         weight_bytes(i).wait_send()
     for e in range(EXCHANGES):
         seq_bytes(e).wait_send()
@@ -526,11 +590,11 @@
             V((rows, heads), F32),
             V((n_head, rows, heads), BF16),
             V((n_head, rows, cols), BF16),
-            V((n_head, owned, n_seq, CAP, cols), BF16),
+            V((n_head, owned, 2, n_seq // 2, CAP, cols), BF16),
             V((owned, n_seq, CAP, cols), BF16),
             V((n_head, rows, hidden), BF16),
-            V((n_head, owned, taken, hidden), BF16),
-            V((owned, n_seq, CAP, cols), BF16),
+            V((n_head, owned, 2, taken // 2, hidden), BF16),
+            V((owned, 2, n_seq // 2, CAP, cols), BF16),
             V((owned, n_seq, CAP, cols), BF16),
             V((rows, cols), F32),
             V((slots, rows), BF16),
@@ -538,8 +602,8 @@
             V((1 + owned, most, 2 * hidden), F32),
             V((1 + owned, most, HD), F32),
             dma((12,)),
-            dma((5,)),
-            dma((5,)),
+            dma((9,)),
+            dma((9,)),
             dma((EXCHANGES,)),
             dma((EXCHANGES,)),
             dma((GATHERS,)),

time: 107 us -> 97.2 us (0.908)
  Pallas kernels: 105 us -> 95.4 us
    pallas_call x1, Pallas kernels: 105 us -> 95.4 us  [shards(): pl.pallas_call(functools.partial(layer_kernel, n_seq, n_head), out_shape=...]
where the time goes in v4:
time: 97.2 us; the launch traced here: 97 us
  Pallas kernels  95.4 us (98%)
  local copies, waits for them, and re-layouts  1.67 us (2%)
    pallas_call x1, Pallas kernels, shards(): pl.pallas_call(functools.partial(layer_kernel, n_seq, n_head), out_shape=...  95.4 us

profile of v4, /device:TPU:1, one launch (start us, length us, event | category | flops | bytes accessed | tf_op | source)
XLA Modules:
  0.0 97.0 jit_solution(13528677050714890231)
XLA Ops:
  0.0 95.4 %shard_map.118 = bf16[512,256]{1,0:T(8,128)(2,1)} custom-call(bf16[512,2048]{1,0:T(8,128)(2,1)} %tok.1, bf16[2048,256]{1,0:T(8,128)(2,1)} %wq.1, bf16[2048,256]{1,0:T(8,128)(2,1)} %wk.1, bf16[2048,256]{1,0:T(8,128)(2,1)} %wv.1, bf16[256,2048]{1,0:T(8,128)(2,1)} %wo.1, bf16[2048,128]{1,0:T(8,128)(2,1)} %sg.1, bf16[2048,128]{1,0:T(8,128)(2,1)} %su.1, ...), custom_call_target="tpu_custom_call" | custom-call | tf_op jit(solution)/shard_map/pallas_call | solution.py:571
  95.4 1.7 %copy.14 = bf16[512,256]{1,0:T(8,128)(2,1)} copy(bf16[512,256]{1,0:T(8,128)(2,1)} %shard_map.118) | data formatting | bytes 524288

commit v5 on v4

--- a/solution.py
+++ b/solution.py
@@ -10,8 +10,6 @@
 HD = 128
 CAP = 16
 NY = 4
-AHEAD = 4
-LOTS = ((0, 0), (0, 1), (1, 0), (1, 1))
 F32 = jnp.float32
 BF16 = jnp.bfloat16
 
@@ -76,17 +74,21 @@
     loads = [
         load(0, tok, x),
         load(1, wq, wqkv.at[:, pl.ds(0, span)]),
-        load(2, wk, wqkv.at[:, pl.ds(span, span)]),
-        load(3, wv, wqkv.at[:, pl.ds(2 * span, span)]),
-        load(4, tok.at[:, col_slice(h, cols)], own),
-        load(5, wo.at[:, col_slice(h, cols)], wo_v.at[h]),
-        load(6, sd.at[:, col_slice(h, cols)], sd_v.at[h]),
-        load(7, ed.at[:, :, col_slice(h, cols)], ed_v.at[h]),
-        load(8, sg, sgu.at[:, pl.ds(0, hidden)]),
-        load(9, su, sgu.at[:, pl.ds(hidden, hidden)]),
-        load(10, eg, egu.at[:, :, pl.ds(0, hidden)]),
-        load(11, eu, egu.at[:, :, pl.ds(hidden, hidden)]),
+        load(1, wk, wqkv.at[:, pl.ds(span, span)]),
+        load(1, wv, wqkv.at[:, pl.ds(2 * span, span)]),
+        load(2, tok.at[:, col_slice(h, cols)], own),
+        load(3, wo.at[:, col_slice(h, cols)], wo_v.at[h]),
+        load(4, sd.at[:, col_slice(h, cols)], sd_v.at[h]),
+        load(5, ed.at[:, :, col_slice(h, cols)], ed_v.at[h]),
+        load(6, sg, sgu.at[:, pl.ds(0, hidden)]),
+        load(6, su, sgu.at[:, pl.ds(hidden, hidden)]),
+        load(7, eg, egu.at[:, :, pl.ds(0, hidden)]),
+        load(7, eu, egu.at[:, :, pl.ds(hidden, hidden)]),
     ]
+
+    def loaded(i):
+        ref = (x, wqkv, own, wo_v.at[h], sd_v.at[h], ed_v.at[h], sgu, egu)[i]
+        load(i, ref, ref).wait()
 
     def seq_peer(t):
         return (s + t) % n_seq
@@ -115,12 +117,15 @@
         n = (wo_v, sd_v)[i].shape[1] // NY
         return pl.ds(pl.multiple_of(lay * n, n), n)
 
+    def ed_lines(i):
+        early = hidden // 4 * 3
+        return pl.ds(0, early) if i == 2 else pl.ds(early, hidden - early)
+
     def weight_copy(i, peer):
         at = col_slice(peer, cols)
-        if i >= 5:
-            e, part = LOTS[i - 5]
-            part = pl.ds(part * (hidden // 2), hidden // 2)
-            src, dst = ed.at[e, part, at], ed_v.at[h, e, part]
+        if i in (2, 5):
+            lines = ed_lines(i)
+            src, dst = ed.at[:, lines, at], ed_v.at[h, :, lines]
         else:
             src, dst = (wo, sd)[i].at[part_of(i), at], (wo_v, sd_v)[i].at[h, part_of(i)]
         return pltpu.make_async_remote_copy(
@@ -129,8 +134,8 @@
 
     def weight_bytes(i):
         some = pl.ds(0, n_head - 1)
-        if i >= 5:
-            ref = ed_v.at[some, 0, pl.ds(0, hidden // 2)]
+        if i in (2, 5):
+            ref = ed_v.at[some, :, ed_lines(i)]
         elif i < 2:
             ref = (wo_v, sd_v)[i].at[some, pl.ds(0, (wo_v, sd_v)[i].shape[1] // NY)]
         else:
@@ -164,12 +169,15 @@
         e = (e - DISPATCH) // 2
         return outb.at[e, peer], rin.at[h, e, s % 2, s // 2]
 
+    def source_of(e):
+        return min(e, DISPATCH) + (e >= RETURN)
+
     def seq_send(e, first, last, stride):
         def one(t, carry):
             peer = seq_peer(t * stride + first)
             src, dst = seq_refs(e, peer)
             pltpu.make_async_remote_copy(
-                src, dst, s_send.at[e], s_recv.at[e], device_id={"seq": peer}
+                src, dst, s_send.at[source_of(e)], s_recv.at[e], device_id={"seq": peer}
             ).start()
             return carry
 
@@ -185,8 +193,16 @@
             count = n_seq // 2 - 1 + e % 2
         ref = ref.at[pl.ds(0, count)]
         return pltpu.make_async_remote_copy(
-            ref, ref, s_send.at[e], s_recv.at[e], device_id={"seq": seq_peer(1)}
+            ref, ref, s_send.at[source_of(e)], s_recv.at[e], device_id={"seq": seq_peer(1)}
         )
+
+    def seq_sent(e):
+        some = pl.ds(0, n_seq - 1)
+        ref = st if e == STATE else pre if e == CARRY else back
+        ref = ref.at[some] if e < DISPATCH else ref.at[:, some]
+        pltpu.make_async_remote_copy(
+            ref, ref, s_send.at[source_of(e)], s_recv.at[e], device_id={"seq": seq_peer(1)}
+        ).wait_send()
 
     parity = s % 2
     middle = rows // 2
@@ -208,42 +224,43 @@
         n = whole.shape[0] // 2
         return whole.at[pl.ds(k * n, n)]
 
+    def buffer_of(g):
+        return (g >= MIDDLE) + (g >= SHARED_HIDDEN) + (g >= ROUTED) + (g >= ROUTED_HIDDEN)
+
     def leg(g, ref, i, target):
         return pltpu.make_async_remote_copy(
-            ref, ref, g_send.at[g], g_recv.at[g, i], device_id={"head": target}
+            ref, ref, g_send.at[buffer_of(g)], g_recv.at[g, i], device_id={"head": target}
         )
 
-    FROM_LEFT, FROM_RIGHT, FROM_TWIN, FAR, TWIN_LEFT, TWIN_RIGHT, TWIN_FAR = range(7)
+    NEAR, FAR, TWIN = range(3)
 
     def arrived(g, i):
-        b = (left, right, partner, far, twin(left), twin(right), twin(far))[i]
-        leg(g, view(g, b), i, partner).wait_recv()
-        return b
+        count = (3, 1, 3)[i]
+        leg(g, view(g, pl.ds(0, count)), i, partner).wait_recv()
+
+    twins = (twin(left), twin(right), twin(far))
 
     def gather_start(g):
-        leg(g, view(g, h), FROM_LEFT, right).start()
-        leg(g, view(g, h), FROM_RIGHT, left).start()
-        leg(g, view(g, h), FROM_TWIN, partner).start()
+        for target in (right, left, partner):
+            leg(g, view(g, h), NEAR, target).start()
 
     def gather_pass(g):
-        arrived(g, FROM_LEFT)
+        arrived(g, NEAR)
         leg(g, half(g, left, 0), FAR, right).start()
-        leg(g, view(g, left), TWIN_LEFT, partner).start()
-        arrived(g, FROM_RIGHT)
         leg(g, half(g, right, 1), FAR, left).start()
-        leg(g, view(g, right), TWIN_RIGHT, partner).start()
+        leg(g, view(g, left), TWIN, partner).start()
+        leg(g, view(g, right), TWIN, partner).start()
 
     def gather_far(g):
         arrived(g, FAR)
-        leg(g, view(g, far), TWIN_FAR, partner).start()
+        leg(g, view(g, far), TWIN, partner).start()
 
     def gather_sent(g):
-        some = pl.ds(0, n_head - 1)
-        ref = view(g, some)
+        ref = (hn, mid, hs, rin, hr)[buffer_of(g)].at[pl.ds(0, n_head - 1)]
         leg(g, ref, 0, partner).wait_send()
 
-    for i in (0, 1, 2, 3):
-        loads[i].wait()
+    loaded(0)
+    loaded(1)
     block = min(256, rows)
 
     def square_sum(ref, at, count):
@@ -309,8 +326,7 @@
 
     weight_start(0)
     weight_start(1)
-    for i in range(5, 5 + AHEAD):
-        weight_start(i)
+    weight_start(2)
     seq_bytes(STATE).wait_recv()
 
     def running(j, total):
@@ -333,11 +349,12 @@
     gather_start(HEADS)
     gather_start(HEADS + 1)
 
-    loads[4].wait()
+    loaded(2)
     res[...] = own[...].astype(F32)
     for k in range(2):
         gather_pass(HEADS + k)
-    loads[5].wait()
+    weight_start(5)
+    loaded(3)
     weight_bytes(3).wait_recv()
 
     def use_heads(k, b):
@@ -346,14 +363,15 @@
 
     for k in range(2):
         use_heads(k, h)
-        use_heads(k, arrived(HEADS + k, FROM_TWIN))
+        use_heads(k, partner)
         use_heads(k, left)
         use_heads(k, right)
     for k in range(2):
         gather_far(HEADS + k)
         use_heads(k, far)
-        for i in (TWIN_LEFT, TWIN_RIGHT, TWIN_FAR):
-            use_heads(k, arrived(HEADS + k, i))
+        arrived(HEADS + k, TWIN)
+        for b in twins:
+            use_heads(k, b)
         at = pl.ds(k * middle, middle)
         mid[h, at, :] = res[at, :].astype(BF16)
         gather_start(MIDDLE + k)
@@ -373,8 +391,7 @@
     weight_bytes(1).wait_recv()
     weight_share(1)
 
-    loads[8].wait()
-    loads[9].wait()
+    loaded(6)
     acc[...] = jnp.zeros_like(acc)
     sq[...] = jnp.zeros_like(sq)
 
@@ -411,18 +428,18 @@
         return (silu(gate) * up).astype(BF16)
 
     near = (left, right)
-    last = (TWIN_LEFT, TWIN_RIGHT, TWIN_FAR)
 
     def begin(g, use):
         use(h)
-        use(arrived(g, FROM_TWIN))
+        use(partner)
         for b in near:
             use(b)
 
     def end(g, use):
         use(far)
-        for i in last:
-            use(arrived(g, i))
+        arrived(g, TWIN)
+        for b in twins:
+            use(b)
 
     def routed(c):
         return functools.partial(use_routed, c)
@@ -438,8 +455,6 @@
     gather_pass(MIDDLE)
     begin(MIDDLE, shared(0))
     gather_pass(MIDDLE + 1)
-    for i in range(5 + AHEAD, 9):
-        weight_start(i)
     seq_bytes(DISPATCH).wait_recv()
     gather_start(ROUTED)
     gather_far(MIDDLE)
@@ -453,8 +468,7 @@
     gather_pass(ROUTED)
     seq_bytes(DISPATCH + 2).wait_recv()
     gather_start(ROUTED + 2)
-    loads[10].wait()
-    loads[11].wait()
+    loaded(7)
     begin(ROUTED, routed(0))
     gather_pass(ROUTED + 1)
     seq_bytes(DISPATCH + 3).wait_recv()
@@ -474,10 +488,10 @@
     end(ROUTED + 2, routed(2))
     hidden_of(2)
 
-    loads[6].wait()
-    loads[7].wait()
-    for i in range(5, 9):
-        weight_bytes(i).wait_recv()
+    loaded(4)
+    loaded(5)
+    weight_bytes(2).wait_recv()
+    weight_bytes(5).wait_recv()
 
     def use_shared(b):
         res[...] += dot(hs[b], sd_v[b])
@@ -496,8 +510,7 @@
             seq_send(RETURN + e, 1, n_seq // 2, 2)
 
     def hidden_end(c):
-        for i in (FROM_TWIN,) + last:
-            arrived(ROUTED_HIDDEN + c, i)
+        arrived(ROUTED_HIDDEN + c, TWIN)
 
     gather_far(ROUTED_HIDDEN)
     gather_pass(ROUTED_HIDDEN + 1)
@@ -525,19 +538,21 @@
     gather_far(SHARED_HIDDEN)
     for b in (h, left, right, far):
         use_shared(b)
-    for i in (FROM_TWIN, TWIN_LEFT, TWIN_RIGHT, TWIN_FAR):
-        use_shared(arrived(SHARED_HIDDEN, i))
+    use_shared(partner)
+    arrived(SHARED_HIDDEN, TWIN)
+    for b in twins:
+        use_shared(b)
     seq_bytes(RETURN).wait_recv()
     res[...] += dot(chosen_t[:, :taken], back[0].reshape(taken, cols))
     seq_bytes(RETURN + 1).wait_recv()
     final = dot(chosen_t[:, taken:], back[1].reshape(taken, cols))
     out[...] = (res[...] + final).astype(BF16)
 
-    for i in (0, 1, 3, 4, 5, 6, 7, 8):
+    for i in range(6):
         weight_bytes(i).wait_send()
-    for e in range(EXCHANGES):
-        seq_bytes(e).wait_send()
-    for g in range(GATHERS):
+    for e in (STATE, CARRY, DISPATCH, RETURN):
+        seq_sent(e)
+    for g in (HEADS, MIDDLE, SHARED_HIDDEN, ROUTED, ROUTED_HIDDEN):
         gather_sent(g)
 
 
@@ -601,13 +616,13 @@
             V((rows, slots), BF16),
             V((1 + owned, most, 2 * hidden), F32),
             V((1 + owned, most, HD), F32),
-            dma((12,)),
-            dma((9,)),
-            dma((9,)),
+            dma((8,)),
+            dma((6,)),
+            dma((6,)),
+            dma((4,)),
             dma((EXCHANGES,)),
-            dma((EXCHANGES,)),
-            dma((GATHERS,)),
-            dma((GATHERS, 7)),
+            dma((5,)),
+            dma((GATHERS, 3)),
         ],
         compiler_params=pltpu.CompilerParams(
             collective_id=0, has_side_effects=True, vmem_limit_bytes=60 * 1024 * 1024

time: 97.2 us -> 94.9 us (0.976)
  Pallas kernels: 95.4 us -> 93.1 us
    pallas_call x1, Pallas kernels: 95.4 us -> 93.1 us  [shards(): pl.pallas_call(functools.partial(layer_kernel, n_seq, n_head), out_shape=...]
where the time goes in v5:
time: 94.9 us; the launch traced here: 94.8 us
  Pallas kernels  93.1 us (98%)
  local copies, waits for them, and re-layouts  1.67 us (2%)
    pallas_call x1, Pallas kernels, shards(): pl.pallas_call(functools.partial(layer_kernel, n_seq, n_head), out_shape=...  93.1 us

profile of v5, /device:TPU:1, one launch (start us, length us, event | category | flops | bytes accessed | tf_op | source)
XLA Modules:
  0.0 94.8 jit_solution(6224345195528326317)
XLA Ops:
  0.0 93.1 %shard_map.118 = bf16[512,256]{1,0:T(8,128)(2,1)} custom-call(bf16[512,2048]{1,0:T(8,128)(2,1)} %tok.1, bf16[2048,256]{1,0:T(8,128)(2,1)} %wq.1, bf16[2048,256]{1,0:T(8,128)(2,1)} %wk.1, bf16[2048,256]{1,0:T(8,128)(2,1)} %wv.1, bf16[256,2048]{1,0:T(8,128)(2,1)} %wo.1, bf16[2048,128]{1,0:T(8,128)(2,1)} %sg.1, bf16[2048,128]{1,0:T(8,128)(2,1)} %su.1, ...), custom_call_target="tpu_custom_call" | custom-call | tf_op jit(solution)/shard_map/pallas_call | solution.py:586
  93.1 1.7 %copy.14 = bf16[512,256]{1,0:T(8,128)(2,1)} copy(bf16[512,256]{1,0:T(8,128)(2,1)} %shard_map.118) | data formatting | bytes 524288

commit v6 on v5

--- a/solution.py
+++ b/solution.py
@@ -535,15 +535,15 @@
 
     weight_bytes(4).wait_recv()
     gather_pass(SHARED_HIDDEN)
+    for b in (h, partner, left, right):
+        use_shared(b)
     gather_far(SHARED_HIDDEN)
-    for b in (h, left, right, far):
-        use_shared(b)
-    use_shared(partner)
+    use_shared(far)
+    seq_bytes(RETURN).wait_recv()
+    res[...] += dot(chosen_t[:, :taken], back[0].reshape(taken, cols))
     arrived(SHARED_HIDDEN, TWIN)
     for b in twins:
         use_shared(b)
-    seq_bytes(RETURN).wait_recv()
-    res[...] += dot(chosen_t[:, :taken], back[0].reshape(taken, cols))
     seq_bytes(RETURN + 1).wait_recv()
     final = dot(chosen_t[:, taken:], back[1].reshape(taken, cols))
     out[...] = (res[...] + final).astype(BF16)

time: 94.9 us -> 94.9 us (level)
  no operation moved by 1% of the time
where the time goes in v6:
time: 94.9 us; the launch traced here: 94.8 us
  Pallas kernels  93.1 us (98%)
  local copies, waits for them, and re-layouts  1.67 us (2%)
    pallas_call x1, Pallas kernels, shards(): pl.pallas_call(functools.partial(layer_kernel, n_seq, n_head), out_shape=...  93.1 us

profile of v6, /device:TPU:1, one launch (start us, length us, event | category | flops | bytes accessed | tf_op | source)
XLA Modules:
  0.0 94.8 jit_solution(14437935250573009506)
XLA Ops:
  0.0 93.1 %shard_map.118 = bf16[512,256]{1,0:T(8,128)(2,1)} custom-call(bf16[512,2048]{1,0:T(8,128)(2,1)} %tok.1, bf16[2048,256]{1,0:T(8,128)(2,1)} %wq.1, bf16[2048,256]{1,0:T(8,128)(2,1)} %wk.1, bf16[2048,256]{1,0:T(8,128)(2,1)} %wv.1, bf16[256,2048]{1,0:T(8,128)(2,1)} %wo.1, bf16[2048,128]{1,0:T(8,128)(2,1)} %sg.1, bf16[2048,128]{1,0:T(8,128)(2,1)} %su.1, ...), custom_call_target="tpu_custom_call" | custom-call | tf_op jit(solution)/shard_map/pallas_call | solution.py:586
  93.1 1.7 %copy.14 = bf16[512,256]{1,0:T(8,128)(2,1)} copy(bf16[512,256]{1,0:T(8,128)(2,1)} %shard_map.118) | data formatting | bytes 524288
